TPU v7x, 256 devices: a whole 4x4x8 slice. The times are simulated.
256 devices in a mesh: rows: 64 (over z_lo, y, x, core), cols: 4 (over z_hi).
Axes of the slice: x: 4, y: 4, z: 8 (z_hi: 4, z_lo: 2; z = z_hi * 2 + z_lo), core: 2. Of those that a mesh axis runs over, the one named last changes fastest.
Arguments:
- design: bfloat16 [256, 1048576], P(None, 'rows'), may hold values from -0.28125 to 0.28125
- targets: bfloat16 [128, 1048576], P('cols', 'rows'), may hold values from -8 to 8
- flip_bits: int32 [2, 1048576], P(None, 'rows'), may hold values from 0 to 1
- listed: int32 [2, 32768], P(None, 'rows'), may hold values from 0 to 16383
- block_order: int32 [2, 64, 16], P(None, 'rows'), may hold values from 0 to 15, each once within a row
Outputs:
- solution: float32 [256, 128], P(None, 'cols')
- residual: float32 [128, 1048576], P('cols', 'rows')
Inputs may be any that keep to these rules, and one draw needn't show every extreme that they name: A group's listed rows are its own rows, counted from its first row; repeats may occur. `block_order`: for each step and group the 16 entries are a permutation.
All inputs are finite; a program needn't handle non-finite values.
Results may differ from a plain program's by a relative error of at most 0.017.
Values sent between devices are 32-bit elements; how exact they have to be, the bound alone decides.
A program may use at most 64 MiB of HBM per device.

v0:
```python
import math

import jax
import jax.numpy as jnp
from jax import lax
from jax.sharding import PartitionSpec as P


def on_device(design, targets, flip_bits, listed, block_order):
    unknowns, rows_here = design.shape
    steps_count = flip_bits.shape[0]
    blocks_count = block_order.shape[2]
    block_len = rows_here // blocks_count
    pick_count = listed.shape[1]
    col_share = unknowns // lax.axis_size("cols")
    inv_root = 1.0 / math.sqrt(block_len)
    keep_scale = math.sqrt(rows_here / pick_count)
    own_rows = lax.dynamic_slice_in_dim(design, lax.axis_index("cols") * col_share, col_share, 0)
    positions = jnp.arange(block_len, dtype=jnp.int32)[:, None]
    block_ids = jnp.arange(blocks_count, dtype=jnp.int32)[:, None]
    unit_eye = jnp.eye(unknowns, dtype=jnp.float32)

    def misfit_of(solution):
        product = lax.dot_general(
            solution.astype(jnp.bfloat16),
            design,
            (((0,), (0,)), ((), ())),
            preferred_element_type=jnp.float32,
        )
        return product - targets.astype(jnp.float32)

    solution = jnp.zeros((unknowns, targets.shape[0]), jnp.float32)
    for step_index in range(steps_count):
        sign_rows = (
            (2 * flip_bits[step_index] - 1).astype(jnp.bfloat16).reshape(blocks_count, block_len)
        )
        chosen = listed[step_index]
        order_now = block_order[step_index, 0]
        target_block = chosen // block_len
        within = chosen % block_len
        source = jnp.sum(
            jnp.where(target_block[None, :] == block_ids, order_now[:, None], 0), axis=0
        )
        parity = jnp.zeros((block_len, pick_count), jnp.int32)
        for bit_index in range(block_len.bit_length() - 1):
            parity = parity ^ positions >> bit_index & 1 & (within[None, :] >> bit_index & 1)
        walsh = (1 - 2 * parity).astype(jnp.bfloat16)
        placed = (source[None, :] == block_ids).astype(jnp.bfloat16)
        table = (placed[:, None, :] * sign_rows[:, :, None] * walsh[None, :, :]).reshape(
            rows_here, pick_count
        )
        mixed_rows = (
            jnp.dot(own_rows, table, preferred_element_type=jnp.float32) * inv_root
        ).astype(jnp.bfloat16)
        summed = lax.psum((mixed_rows.astype(jnp.float32) * keep_scale)[None], "rows")
        whole_sketch = lax.all_gather(summed, "cols", axis=1, tiled=True)
        gram_stack = jnp.einsum(
            "npm,nqm->npq", whole_sketch, whole_sketch, precision=lax.Precision.HIGHEST
        )
        shift = jnp.trace(gram_stack, axis1=1, axis2=2) / unknowns
        gram_now = (gram_stack + shift[:, None, None] * unit_eye[None])[0]
        if step_index == 0:
            misfit_half = -targets
        else:
            misfit_half = misfit_of(solution).astype(jnp.bfloat16)
        local_grad = lax.dot_general(
            design, misfit_half, (((1,), (1,)), ((), ())), preferred_element_type=jnp.float32
        )
        gradient = lax.psum(local_grad, "rows")
        factor = jnp.linalg.cholesky(gram_now)
        solution = solution - jax.scipy.linalg.cho_solve((factor, True), gradient)
    return (solution, misfit_of(solution))


def solution(mesh):
    return jax.shard_map(
        on_device,
        mesh=mesh,
        in_specs=(
            P(None, "rows"),
            P("cols", "rows"),
            P(None, "rows"),
            P(None, "rows"),
            P(None, "rows", None),
        ),
        out_specs=(P(None, "cols"), P("cols", "rows")),
        check_vma=False,
    )
```

profile of v0, /device:TPU:1, one launch (start us, length us, event | category | flops | bytes accessed | tf_op | source)
XLA Modules:
  0.0 999.2 jit_solution(7467058959739676185)
XLA Ops:
  7.3 0.8 and_select_fusion.3
  8.9 1.4 convert_reduce_fusion.1
  10.4 2.0 subtract_convert_fusion.1
  12.4 2.8 bitcast_multiply_fusion.2
  15.2 3.7 fusion.32
  18.9 2.0 subtract_convert_fusion
  20.9 2.8 bitcast_multiply_fusion
  23.7 3.7 fusion.20
  27.4 6.0 fusion.35
  33.4 275.8 %psum.29 = f32[256,32]{0,1:T(8,128)S(1)} all-reduce(f32[256,32]{0,1:T(8,128)S(1)} %fusion.35), channel_id=1, replica_groups=mesh['rows'=64,'cols'=4] {'rows'}, use_global_device_ids=true, to_apply=%region_7.9 | all-reduce | flops 8192 | bytes 65536 | tf_op jit(solution)/shard_map/psum | solution.py:69
  309.2 235.2 %all-reduce.4.cloned.1.call-done = (f32[1,64,512]{2,1,0:T(8,128)}, f32[1,64,512]{2,1,0:T(8,128)}) async-done(((f32[1,64,512]{2,1,0:T(8,128)}, f32[1,64,512]{2,1,0:T(8,128)}), (f32[1,64,512]{2,1,0:T(8,128)}, f32[1,64,512]{2,1,0:T(8,128)})) %all-reduce.4.cloned.1.call-update) | async-done | bytes 262160 | tf_op jit(solution)/shard_map/psum | solution.py:55
  544.4 16.0 %all_gather.6 = f32[1,256,512]{2,1,0:T(8,128)S(1)} all-gather(f32[1,64,512]{2,1,0:T(8,128)} %get-tuple-element.39), channel_id=1, replica_groups=mesh['rows'=64,'cols'=4] {'cols'}, dimensions={1}, use_global_device_ids=true | all-gather | bytes 655360 | tf_op jit(solution)/shard_map/all_gather | solution.py:56
  560.4 1.2 select_reduce_fusion.1
  562.5 11.7 %cholesky.130 = f32[128,128]{1,0:T(8,128)S(1)} custom-call(f32[128,128]{1,0:T(8,128)S(1)} %cholesky.194), custom_call_target="Cholesky" | custom-call | tf_op jit(solution)/shard_map/jit(cholesky)/cholesky | solution.py:70
  574.3 9.8 custom-call.15
  584.6 11.7 %cholesky.147 = f32[128,128]{1,0:T(8,128)S(1)} custom-call(f32[128,128]{1,0:T(8,128)S(1)} %convolution_subtract_fusion.3), custom_call_target="Cholesky" | custom-call | tf_op jit(solution)/shard_map/jit(cholesky)/cholesky | solution.py:70
  598.9 4.0 while.4
  599.8 1.3 bitcast_dynamic-update-slice_fusion.4
  601.7 1.3 bitcast_dynamic-update-slice_fusion.4
  603.0 19.7 %custom-call.16 = f32[2,128,128]{1,2,0:T(8,128)S(1)} custom-call(f32[2,128,128]{2,1,0:T(8,128)S(1)} %get-tuple-element.18), custom_call_target="InvertDiagBlocksLowerTriangular" | custom-call | tf_op jit(solution)/shard_map/jit(_cho_solve)/triangular_solve | solution.py:71
  624.0 9.9 convolution_bitcast_fusion
  633.9 274.0 %psum.31 = f32[256,32]{0,1:T(8,128)S(1)} all-reduce(f32[256,32]{0,1:T(8,128)S(1)} %convolution_bitcast_fusion), channel_id=1, replica_groups=mesh['rows'=64,'cols'=4] {'rows'}, use_global_device_ids=true, to_apply=%region_11.14 | all-reduce | flops 8192 | bytes 65536 | tf_op jit(solution)/shard_map/psum | solution.py:69
  907.9 13.7 %all_gather.7 = f32[1,256,512]{2,1,0:T(8,128)S(1)} all-gather(f32[1,64,512]{2,1,0:T(8,128)S(1)} %copy-done.2), channel_id=1, replica_groups=mesh['rows'=64,'cols'=4] {'cols'}, dimensions={1}, use_global_device_ids=true | all-gather | bytes 655360 | tf_op jit(solution)/shard_map/all_gather | solution.py:56
  921.5 1.2 select_reduce_fusion
  923.6 11.7 %cholesky.164 = f32[128,128]{1,0:T(8,128)S(1)} custom-call(f32[128,128]{1,0:T(8,128)S(1)} %cholesky.197), custom_call_target="Cholesky" | custom-call | tf_op jit(solution)/shard_map/jit(cholesky)/cholesky | solution.py:70
  935.4 9.8 custom-call.17
  945.7 11.7 %cholesky.181 = f32[128,128]{1,0:T(8,128)S(1)} custom-call(f32[128,128]{1,0:T(8,128)S(1)} %convolution_subtract_fusion.2), custom_call_target="Cholesky" | custom-call | tf_op jit(solution)/shard_map/jit(cholesky)/cholesky | solution.py:70
  960.2 4.4 while.5
  961.1 1.4 bitcast_dynamic-update-slice_fusion.5
  963.1 1.4 bitcast_dynamic-update-slice_fusion.5
  964.6 19.7 %custom-call.18 = f32[2,128,128]{1,2,0:T(8,128)S(1)} custom-call(f32[2,128,128]{2,1,0:T(8,128)S(1)} %get-tuple-element.19), custom_call_target="InvertDiagBlocksLowerTriangular" | custom-call | tf_op jit(solution)/shard_map/jit(_cho_solve)/triangular_solve | solution.py:71
  985.7 6.3 convolution_subtract_fusion
  (74 shorter events, 10.2 us)
Async XLA Ops:
  7.2 537.2 %all-reduce.4.cloned.1.call-start = ((), (), s32[]{:S(2)}) async-start(), calls=%async_computation | async-start | bytes 524288 | tf_op jit(solution)/shard_map/psum | solution.py:55
  10.3 4.9 slice-start
  12.4 2.8 slice-start.1
  23.7 3.7 copy-start
  624.0 283.9 %copy-start.2 = (f32[1,64,512]{2,1,0:T(8,128)S(1)}, f32[1,64,512]{2,1,0:T(8,128)}, u32[]{:S(2)}) copy-start(f32[1,64,512]{2,1,0:T(8,128)} %get-tuple-element.38) | copy-start | bytes 393220
  985.6 6.3 copy-start.1
Sparse Core Ops, SparseCore 0:
  27.5 516.8 all-reduce.3
where the time goes:
time: 1010 us; the launch traced here: 999 us
  blocking collectives  580 us (57%)
  waiting for transfers between devices  235 us (23%)
  other arithmetic  121 us (12%)
  matrix products  35.3 us (3%)
  between operations  18.9 us (2%)
    psum x2, blocking collectives, on_device(): gradient = lax.psum(local_grad, 'rows')  550 us
    psum x1, waiting for transfers between devices, on_device(): lax.psum((mixed_rows.astype(jnp.float32) * keep_scale)[None], 'rows')  235 us
    another operation x14, other arithmetic, on_device(): factor = jnp.linalg.cholesky(gram_now)  69.2 us
    another operation x5, other arithmetic, on_device(): solution = solution - jax.scipy.linalg.cho_solve((factor, True), gradient)  39.4 us
    all_gather x2, blocking collectives, on_device(): whole_sketch = lax.all_gather(summed, 'cols', axis=1, tiled=True)  29.7 us
  transfers between devices with their start and end apart: 1, of which 1 were waited for; matrix products, arithmetic and copies ran while one was open for 1% of the time, Pallas kernels for 0%

commit v1 on v0

v1 whole, which is shorter than its diff:
```python
import functools
import math

import jax
import jax.numpy as jnp
from jax import lax
from jax.experimental import pallas as pl
from jax.experimental.pallas import tpu as pltpu
from jax.sharding import PartitionSpec as P

MESH = pl.DeviceIdType.MESH
F32 = jnp.float32
BF16 = jnp.bfloat16
NB = 32
NT = (((1,), (1,)), ((), ()))
TN = (((0,), (0,)), ((), ()))
HIGHEST = lax.Precision.HIGHEST


def split(x):
    hi = x.astype(BF16)
    return hi, (x - hi.astype(F32)).astype(BF16)


def kernel(
    order_ref,
    design_ref,
    targets_ref,
    flips_ref,
    listed_ref,
    out_ref,
    dv,
    tv,
    fv,
    lv,
    walsh,
    srcs,
    lhs_a,
    lhs_b,
    acc,
    xs,
    xe,
    rs_s,
    rs_e,
    sf,
    ef,
    mat,
    gmat,
    bt,
    xsend,
    xrecv,
    ysend,
    yrecv,
    in_sems,
    send_sems,
    recv_sems,
):
    unknowns = dv.shape[0]
    rows_here = dv.shape[1]
    block_len = walsh.shape[1]
    blocks = rows_here // block_len
    steps = 2
    picks = 128
    inv_root = 1.0 / math.sqrt(block_len)
    keep_scale = math.sqrt(rows_here / listed_ref.shape[1])
    row = lax.axis_index("rows")
    col = lax.axis_index("cols")
    core = row % 2
    xy = (row // 2) % 16
    z_lo = row // 32
    z = col * 2 + z_lo

    def chunk_copy(b):
        lanes = pl.ds(b * block_len, block_len)
        return pltpu.make_async_copy(design_ref.at[:, lanes], dv.at[:, lanes], in_sems.at[b])

    small = (
        pltpu.make_async_copy(listed_ref, lv, in_sems.at[blocks]),
        pltpu.make_async_copy(flips_ref, fv, in_sems.at[blocks + 1]),
        pltpu.make_async_copy(targets_ref, tv, in_sems.at[blocks + 2]),
    )
    small[0].start()
    small[1].start()
    chunk_copy(0).start()
    small[2].start()
    for b in range(1, blocks):
        chunk_copy(b).start()

    barrier = pltpu.get_barrier_semaphore()

    @pl.loop(1, 64)
    def _(k):
        pl.semaphore_signal(
            barrier, inc=1, device_id=((row + k) % 64, col), device_id_type=MESH
        )

    def z_peer(k):
        other = (z + k) % 8
        return ((other % 2) * 32 + row % 32, other // 2)

    for k in range(1, 8):

        @pl.when(((z + k) % 8) // 2 != col)
        def _():
            pl.semaphore_signal(barrier, inc=1, device_id=z_peer(k), device_id_type=MESH)

    small[0].wait()
    picked = lv[:, pl.ds(pl.multiple_of(col * picks, picks), picks)]
    eye = lax.broadcasted_iota(jnp.int32, (picks, picks), 0) == lax.broadcasted_iota(
        jnp.int32, (picks, picks), 1
    )
    for t in range(steps):
        line = picked[t : t + 1, :]
        target_block = line // block_len
        source = jnp.zeros_like(line)
        for b in range(blocks):
            source = jnp.where(target_block == b, order_ref[t, b], source)
        code = (source * block_len + line % block_len).astype(F32)
        column = jnp.sum(
            jnp.where(eye, jnp.broadcast_to(code, (picks, picks)), 0.0), axis=1, keepdims=True
        ).astype(jnp.int32)
        srcs[t * picks : (t + 1) * picks, :] = jnp.broadcast_to(column // block_len, (picks, 128))
        within = column % block_len
        for h in range(block_len // 128):
            places = lax.broadcasted_iota(jnp.int32, (picks, 128), 1) + h * 128
            bits = within & places
            bits = bits ^ (bits >> 8)
            bits = bits ^ (bits >> 4)
            bits = bits ^ (bits >> 2)
            bits = (bits ^ (bits >> 1)) & 1
            walsh[t * picks : (t + 1) * picks, h * 128 : (h + 1) * 128] = (
                (1 - 2 * bits).astype(F32).astype(BF16)
            )
    small[1].wait()
    small[2].wait()
    acc[...] = jnp.zeros_like(acc)

    def block_terms(b, lhs):
        lanes = pl.ds(pl.multiple_of(b * block_len, block_len), block_len)
        pltpu.make_async_copy(
            design_ref.at[:, lanes], dv.at[:, lanes], in_sems.at[b]
        ).wait()
        for t in range(steps):
            own = slice(t * picks, (t + 1) * picks)
            sign = (2 * fv[t : t + 1, lanes] - 1).astype(F32).astype(BF16)
            chosen = jnp.where(srcs[own, 0:128] == b, 1.0, 0.0).astype(BF16)
            for h in range(block_len // 128):
                part = slice(h * 128, (h + 1) * 128)
                lhs[own, part] = walsh[own, part] * chosen * sign[:, part]
        first = steps * picks
        lhs[first : first + 64, :] = dv[pl.ds(pl.multiple_of(col * 64, 64), 64), lanes]
        lhs[first + 64 : first + 96, :] = tv[:, lanes]
        acc[...] += lax.dot_general(lhs[...], dv[:, lanes], NT, preferred_element_type=F32)

    @pl.loop(0, blocks // 2)
    def _(pair):
        block_terms(2 * pair, lhs_a)
        block_terms(2 * pair + 1, lhs_b)

    for half in range(2):
        lanes = slice(half * 128, (half + 1) * 128)
        for rb in range(16):
            for t in range(steps):
                first = t * picks + rb * 8
                tile = (acc[first : first + 8, lanes] * inv_root).astype(BF16)
                xs[2 * (half * 16 + rb) + t] = tile.astype(F32) * keep_scale
            first = 2 * picks + rb * 4
            xe[2 * (half * 16 + rb) + 1] = acc[first : first + 4, lanes]
            if rb < 8:
                first = 2 * picks + 64 + rb * 4
                xe[2 * (half * 16 + rb)] = acc[first : first + 4, lanes]
            else:
                xe[2 * (half * 16 + rb)] = jnp.zeros((4, 128), F32)

    pl.semaphore_wait(barrier, 63 + 6)

    def remote(src, dst, stage, peer):
        return pltpu.make_async_remote_copy(
            src_ref=src,
            dst_ref=dst,
            send_sem=send_sems.at[stage],
            recv_sem=recv_sems.at[stage],
            device_id=peer,
            device_id_type=MESH,
        )

    def scatter(src, dst, stage):
        @pl.loop(1, 64)
        def _(k):
            peer = (row + k) % 64
            remote(src.at[peer], dst.at[k - 1], stage, (peer, col)).start()

    def gather_z(full, stage):
        @pl.loop(1, 8)
        def _(k):
            place = full.at[z, xy]
            remote(place, place, stage, z_peer(k)).start()

    def gather_xy(full, stage):
        @pl.loop(1, 16)
        def _(k):
            place = full.at[:, xy]
            peer = z_lo * 32 + ((xy + k) % 16) * 2 + core
            remote(place, place, stage, (peer, col)).start()

    def all_of(buffer, stage):
        return remote(buffer, buffer, stage, (row, col))

    def total(own, parts):
        sums = [own]
        for lead in range(3):
            sums.append(parts[lead])
        for index in range(3, 63):
            sums[index % 4] = sums[index % 4] + parts[index]
        return (sums[0] + sums[1]) + (sums[2] + sums[3])

    scatter(xs, rs_s, 0)
    scatter(xe, rs_e, 1)
    all_of(rs_s, 0).wait_recv()
    sf[z, xy] = total(xs[row], rs_s)
    gather_z(sf, 2)
    all_of(rs_e, 1).wait_recv()
    ef[z, xy] = total(xe[row], rs_e)
    gather_z(ef, 3)
    all_of(rs_s.at[0:7], 2).wait_recv()
    gather_xy(sf, 4)
    all_of(rs_e.at[0:7], 3).wait_recv()
    gather_xy(ef, 5)
    all_of(sf.at[:, 0:15], 4).wait_recv()

    squares = jnp.zeros((8, 128), F32)
    halves = []
    for half in range(2):
        parts = [sf[2 * c + half].reshape(picks, 128) for c in range(4)]
        halves.append(jnp.concatenate(parts, axis=0))
    sketch = jnp.concatenate(halves, axis=1)
    for first in range(0, 512, 8):
        for lane in range(0, 256, 128):
            piece = sketch[first : first + 8, lane : lane + 128]
            squares = squares + piece * piece
    hi, lo = split(sketch)
    gram = lax.dot_general(hi, hi, TN, preferred_element_type=F32)
    gram = gram + lax.dot_general(hi, lo, TN, preferred_element_type=F32)
    gram = gram + lax.dot_general(lo, hi, TN, preferred_element_type=F32)
    shift = jnp.sum(squares) / unknowns
    diagonal = lax.broadcasted_iota(jnp.int32, (unknowns, unknowns), 0) == lax.broadcasted_iota(
        jnp.int32, (unknowns, unknowns), 1
    )
    mat[...] = gram + jnp.where(diagonal, shift, 0.0)

    lane_ids = lax.broadcasted_iota(jnp.int32, (NB, unknowns), 1)
    row_ids = lax.broadcasted_iota(jnp.int32, (NB, unknowns), 0)
    for k0 in range(0, unknowns, NB):
        band = slice(k0, k0 + NB)
        panel = mat[band, :]
        signed = jnp.where(lane_ids < k0, -panel, panel)
        left_hi, left_lo = split(signed)
        left = jnp.concatenate([left_hi, left_hi, left_lo], axis=0)
        for j in range(NB):
            c = k0 + j
            column = panel[:, c : c + 1]
            inverse = 1.0 / panel[j : j + 1, c : c + 1]
            cleared = jnp.where(lane_ids == c, 0.0, panel)
            line = jnp.where(lane_ids[0:1] == c, 1.0, panel[j : j + 1, :]) * inverse
            panel = jnp.where(row_ids == j, line, cleared - column * line)
        right_hi, right_lo = split(panel)
        right = jnp.concatenate([right_hi, right_lo, right_hi], axis=0)
        update = lax.dot_general(left, right, TN, preferred_element_type=F32)
        for other in range(0, unknowns, NB):
            here = slice(other, other + NB)
            if other == k0:
                mat[here, :] = panel
            else:
                kept = jnp.where((lane_ids >= k0) & (lane_ids < k0 + NB), 0.0, mat[here, :])
                mat[here, :] = kept - update[here, :]

    all_of(ef.at[:, 0:15], 5).wait_recv()

    @pl.when(core == 0)
    def _():
        for half in range(2):
            for rb in range(8):
                bt[rb * 4 : rb * 4 + 4, half * 128 : (half + 1) * 128] = ef[2 * col + half, rb]
        first = jnp.dot(bt[...], mat[...], precision=HIGHEST, preferred_element_type=F32)
        xsend[0:32, :] = first
        xsend[32:64, :] = bt[...]
        handed = remote(xsend, xrecv, 6, (row + 1, col))
        handed.start()
        remote(ysend, yrecv, 7, (row + 1, col)).wait_recv()
        out_ref[...] = yrecv[...]
        handed.wait_send()

    @pl.when(core == 1)
    def _():
        for c in range(4):
            for half in range(2):
                for rb in range(16):
                    first = c * 64 + rb * 4
                    gmat[first : first + 4, half * 128 : (half + 1) * 128] = ef[2 * c + half, rb]
        remote(xsend, xrecv, 6, (row - 1, col)).wait_recv()
        start = xrecv[0:32, :]
        rounded = start.astype(BF16).astype(F32)
        gradient = jnp.dot(rounded, gmat[...], precision=HIGHEST, preferred_element_type=F32)
        gradient = gradient - xrecv[32:64, :]
        moved = start - jnp.dot(gradient, mat[...], precision=HIGHEST, preferred_element_type=F32)
        ysend[...] = moved
        handed = remote(ysend, yrecv, 7, (row - 1, col))
        handed.start()
        out_ref[...] = moved
        handed.wait_send()

    all_of(rs_s, 0).wait_send()
    all_of(rs_e, 1).wait_send()
    all_of(rs_s.at[0:7], 2).wait_send()
    all_of(rs_e.at[0:7], 3).wait_send()
    all_of(sf.at[:, 0:15], 4).wait_send()
    all_of(ef.at[:, 0:15], 5).wait_send()


def on_device(design, targets, flip_bits, listed, block_order):
    unknowns, rows_here = design.shape
    block_len = rows_here // block_order.shape[2]
    rhs = targets.shape[0]
    any_space = pl.BlockSpec(memory_space=pl.ANY)
    solved = pl.pallas_call(
        kernel,
        out_shape=jax.ShapeDtypeStruct((rhs, unknowns), F32),
        in_specs=[pl.BlockSpec(memory_space=pltpu.SMEM)] + [any_space] * 4,
        out_specs=pl.BlockSpec(memory_space=pltpu.VMEM),
        scratch_shapes=[
            pltpu.VMEM((unknowns, rows_here), BF16),
            pltpu.VMEM((rhs, rows_here), BF16),
            pltpu.VMEM((2, rows_here), jnp.int32),
            pltpu.VMEM((2, 512), jnp.int32),
            pltpu.VMEM((256, block_len), BF16),
            pltpu.VMEM((256, 128), jnp.int32),
            pltpu.VMEM((352, block_len), BF16),
            pltpu.VMEM((352, block_len), BF16),
            pltpu.VMEM((352, unknowns), F32),
            pltpu.VMEM((64, 8, 128), F32),
            pltpu.VMEM((64, 4, 128), F32),
            pltpu.VMEM((63, 8, 128), F32),
            pltpu.VMEM((63, 4, 128), F32),
            pltpu.VMEM((8, 16, 8, 128), F32),
            pltpu.VMEM((8, 16, 4, 128), F32),
            pltpu.VMEM((unknowns, unknowns), F32),
            pltpu.VMEM((unknowns, unknowns), F32),
            pltpu.VMEM((rhs, unknowns), F32),
            pltpu.VMEM((2 * rhs, unknowns), F32),
            pltpu.VMEM((2 * rhs, unknowns), F32),
            pltpu.VMEM((rhs, unknowns), F32),
            pltpu.VMEM((rhs, unknowns), F32),
            pltpu.SemaphoreType.DMA((block_order.shape[2] + 3,)),
            pltpu.SemaphoreType.DMA((8,)),
            pltpu.SemaphoreType.DMA((8,)),
        ],
        compiler_params=pltpu.CompilerParams(
            collective_id=0, has_side_effects=True, vmem_limit_bytes=40 * 1024 * 1024
        ),
        name="sketch_solve",
    )(block_order.reshape(2, block_order.shape[2]), design, targets, flip_bits, listed)
    residual = jnp.dot(
        solved.astype(BF16), design, preferred_element_type=F32
    ) - targets.astype(F32)
    return (solved.T, residual)


def solution(mesh):
    return jax.shard_map(
        on_device,
        mesh=mesh,
        in_specs=(
            P(None, "rows"),
            P("cols", "rows"),
            P(None, "rows"),
            P(None, "rows"),
            P(None, "rows", None),
        ),
        out_specs=(P(None, "cols"), P("cols", "rows")),
        check_vma=False,
    )
```

time: 1010 us -> 78.8 us (0.08); the launches traced: 999 us -> 78.6 us
  blocking collectives: 580 us -> 0 us
  waiting for transfers between devices: 235 us -> 0 us
  other arithmetic: 121 us -> 0 us
  Pallas kernels: 0 us -> 67.6 us
  matrix products: 35.3 us -> 2.87 us
  between operations: 18.9 us -> 0.65 us
    psum x2 -> x0, blocking collectives: 550 us -> none  [on_device(): gradient = lax.psum(local_grad, 'rows')]
    psum x1 -> x0, waiting for transfers between devices: 235 us -> none  [on_device(): lax.psum((mixed_rows.astype(jnp.float32) * keep_scale)[None], 'rows')]
    another operation x19 -> x0, other arithmetic: 109 us -> none  [the longest x14 69.2 us: on_device(): factor = jnp.linalg.cholesky(gram_now)]
    pallas_call x0 -> x1, Pallas kernels: none -> 67.6 us  [on_device(): pl.pallas_call(kernel, out_shape=jax.ShapeDtypeStruct((rhs, unknowns), F3...]
    all_gather x2 -> x0, blocking collectives: 29.7 us -> none  [on_device(): whole_sketch = lax.all_gather(summed, 'cols', axis=1, tiled=True)]
    dot_general x7 -> x1, matrix products: 31.8 us -> 2.87 us  [on_device(): jnp.dot(solved.astype(BF16), design, preferred_element_type=F32)]
  transfers between devices with their start and end apart: 1 -> 0, of which waited for: 1 -> 0; matrix products, arithmetic and copies ran while one was open for 1% -> 0% of each run, Pallas kernels for 0% -> 0%
where the time goes in v1:
time: 78.8 us; the launch traced here: 78.6 us
  Pallas kernels  67.6 us (86%)
  local copies, waits for them, and re-layouts  7.48 us (9%)
  matrix products  2.87 us (4%)
    pallas_call x1, Pallas kernels, on_device(): pl.pallas_call(kernel, out_shape=jax.ShapeDtypeStruct((rhs, unknowns), F3...  67.6 us
    unnamed x11, local copies, waits for them, and re-layouts  7.48 us
    dot_general x1, matrix products, on_device(): jnp.dot(solved.astype(BF16), design, preferred_element_type=F32)  2.87 us

profile of v1, /device:TPU:1, one launch (start us, length us, event | category | flops | bytes accessed | tf_op | source)
XLA Modules:
  0.0 78.6 jit_solution(15061785390873911341)
XLA Ops:
  0.6 0.0 copy-start
  0.6 3.4 %copy-done = bf16[256,16384]{1,0:T(8,128)(2,1)S(1)} copy-done((bf16[256,16384]{1,0:T(8,128)(2,1)S(1)}, bf16[256,16384]{1,0:T(8,128)(2,1)}, u32[]{:S(2)}) %copy-start) | copy-done | bytes 8388632
  4.0 0.0 copy-start.1
  4.0 1.2 %copy-done.1 = bf16[32,16384]{1,0:T(8,128)(2,1)S(1)} copy-done((bf16[32,16384]{1,0:T(8,128)(2,1)S(1)}, bf16[32,16384]{1,0:T(8,128)(2,1)}, u32[]{:S(2)}) %copy-start.1) | copy-done | bytes 1048600
  5.2 0.0 copy-start.2
  5.2 0.9 %copy-done.2 = s32[2,16384]{1,0:T(2,128)S(1)} copy-done((s32[2,16384]{1,0:T(2,128)S(1)}, s32[2,16384]{1,0:T(2,128)}, u32[]{:S(2)}) %copy-start.2) | copy-done | bytes 131096
  6.1 0.0 copy-start.3
  6.1 0.7 copy-done.3
  6.8 0.0 copy-start.4
  6.8 0.7 copy-done.4
  7.5 67.6 %sketch_solve.1 = f32[32,256]{1,0:T(8,128)S(1)} custom-call(s32[2,16]{1,0:T(2,128)S(1)} %bitcast.4, bf16[256,16384]{1,0:T(8,128)(2,1)S(1)} %copy-done, bf16[32,16384]{1,0:T(8,128)(2,1)S(1)} %copy-done.1, s32[2,16384]{1,0:T(2,128)S(1)} %copy-done.2, s32[2,512]{1,0:T(2,128)S(1)} %copy-done.3), custom_call_target="tpu_custom_call" | custom-call | tf_op jit(solution)/shard_map/sketch_solve/pallas_call | solution.py:325
  75.1 2.9 %convolution_subtract_fusion = f32[32,16384]{1,0:T(8,128)} fusion(bf16[256,16384]{1,0:T(8,128)(2,1)S(1)} %copy-done, bf16[32,16384]{1,0:T(8,128)(2,1)S(1)} %copy-done.1, f32[32,256]{1,0:T(8,128)S(1)} %sketch_solve.1), kind=kOutput, calls=%fused_computation | convolution fusion | flops 269492224 | bytes 11567104 | tf_op jit(solution)/shard_map/dot_general | solution.py:362
  78.0 0.6 copy.8
Async XLA Ops:
  0.6 3.4 %copy-start = (bf16[256,16384]{1,0:T(8,128)(2,1)S(1)}, bf16[256,16384]{1,0:T(8,128)(2,1)}, u32[]{:S(2)}) copy-start(bf16[256,16384]{1,0:T(8,128)(2,1)} %design_ref.1) | copy-start | bytes 25165828
  4.0 1.2 %copy-start.1 = (bf16[32,16384]{1,0:T(8,128)(2,1)S(1)}, bf16[32,16384]{1,0:T(8,128)(2,1)}, u32[]{:S(2)}) copy-start(bf16[32,16384]{1,0:T(8,128)(2,1)} %targets_ref.1) | copy-start | bytes 3145732
  5.2 0.9 %copy-start.2 = (s32[2,16384]{1,0:T(2,128)S(1)}, s32[2,16384]{1,0:T(2,128)}, u32[]{:S(2)}) copy-start(s32[2,16384]{1,0:T(2,128)} %flips_ref.1) | copy-start | bytes 393220
  6.1 0.7 copy-start.3
  6.8 0.7 copy-start.4

commit v2 on v1

--- a/solution.py
+++ b/solution.py
@@ -20,6 +20,100 @@
 def split(x):
     hi = x.astype(BF16)
     return hi, (x - hi.astype(F32)).astype(BF16)
+
+
+def lane_of(tile, c):
+    return jnp.broadcast_to(tile[:, c : c + 1], (8, 128))
+
+
+def row_of(tile, j):
+    return jnp.broadcast_to(tile[j : j + 1, :], (8, 128))
+
+
+def tree(terms):
+    while len(terms) > 1:
+        paired = [terms[i] + terms[i + 1] for i in range(0, len(terms) - 1, 2)]
+        terms = paired + ([terms[-1]] if len(terms) % 2 else [])
+    return terms[0]
+
+
+def small_inverse(cols, sub):
+    for q in range(0, 8, 2):
+        a, b, c = row_of(cols[q], q), row_of(cols[q + 1], q), row_of(cols[q + 1], q + 1)
+        r = 1.0 / (a * c - b * b)
+        p00, p01, p11 = c * r, -b * r, a * r
+        w0 = -(cols[q] * p00 + cols[q + 1] * p01)
+        w1 = -(cols[q] * p01 + cols[q + 1] * p11)
+        w0 = jnp.where(sub == q, p00, jnp.where(sub == q + 1, p01, w0))
+        w1 = jnp.where(sub == q, p01, jnp.where(sub == q + 1, p11, w1))
+        fresh = []
+        for j in range(8):
+            if j == q:
+                fresh.append(w0)
+            elif j == q + 1:
+                fresh.append(w1)
+            else:
+                kept = jnp.where((sub == q) | (sub == q + 1), 0.0, cols[j])
+                fresh.append(kept + (w0 * row_of(cols[j], q) + w1 * row_of(cols[j], q + 1)))
+        cols = fresh
+    return cols
+
+
+def eliminate(tiles, k0, sub, lane):
+    home = k0 // 128
+    groups = NB // 8
+    for s in range(groups):
+        c0 = k0 + 8 * s - 128 * home
+        cols = [[lane_of(tiles[g][home], c0 + j) for g in range(groups)] for j in range(8)]
+        inverse = small_inverse([cols[j][s] for j in range(8)], sub)
+        inside = (lane >= c0) & (lane < c0 + 8)
+        unit = jnp.where(lane == sub + c0, 1.0, 0.0)
+        lead = [jnp.where(inside, unit, t) if h == home else t for h, t in enumerate(tiles[s])]
+        fresh = [tree([inverse[j] * row_of(lead[h], j) for j in range(8)]) for h in range(2)]
+        rows = [[row_of(fresh[h], j) for j in range(8)] for h in range(2)]
+        after = []
+        for g in range(groups):
+            if g == s:
+                after.append(fresh)
+                continue
+            line = []
+            for h in range(2):
+                kept = jnp.where(inside, 0.0, tiles[g][h]) if h == home else tiles[g][h]
+                line.append(kept - tree([cols[j][g] * rows[h][j] for j in range(8)]))
+            after.append(line)
+        tiles = after
+    return tiles
+
+
+def invert(mat):
+    n = mat.shape[0]
+    sub = lax.broadcasted_iota(jnp.int32, (8, 128), 0)
+    lane = lax.broadcasted_iota(jnp.int32, (8, 128), 1)
+    wide = lax.broadcasted_iota(jnp.int32, (NB, n), 1)
+    panel = mat[0:NB, :]
+    for k0 in range(0, n, NB):
+        k1 = k0 + NB
+        left_hi, left_lo = split(jnp.where(wide < k0, -panel, panel))
+        left = jnp.concatenate([left_hi, left_hi, left_lo], axis=0)
+        tiles = [
+            [panel[8 * g : 8 * g + 8, 128 * h : 128 * h + 128] for h in range(2)]
+            for g in range(NB // 8)
+        ]
+        tiles = eliminate(tiles, k0, sub, lane)
+        done = jnp.concatenate([jnp.concatenate(t, axis=1) for t in tiles], axis=0)
+        right_hi, right_lo = split(done)
+        right = jnp.concatenate([right_hi, right_lo, right_hi], axis=0)
+        inside = (wide >= k0) & (wide < k1)
+        if k1 < n:
+            first = lax.dot_general(left[:, k1 : k1 + NB], right, TN, preferred_element_type=F32)
+            panel = jnp.where(inside, 0.0, mat[k1 : k1 + NB, :]) - first
+        update = lax.dot_general(left, right, TN, preferred_element_type=F32)
+        for other in range(0, n, NB):
+            here = slice(other, other + NB)
+            if other == k0:
+                mat[here, :] = done
+            elif other != k1:
+                mat[here, :] = jnp.where(inside, 0.0, mat[here, :]) - update[here, :]
 
 
 def kernel(
@@ -31,13 +125,14 @@
     out_ref,
     dv,
     tv,
+    order,
     fv,
     lv,
     walsh,
     srcs,
-    lhs_a,
-    lhs_b,
+    lhs,
     acc,
+    acc_e,
     xs,
     xe,
     rs_s,
@@ -75,24 +170,20 @@
         return pltpu.make_async_copy(design_ref.at[:, lanes], dv.at[:, lanes], in_sems.at[b])
 
     small = (
+        pltpu.make_async_copy(order_ref, order, in_sems.at[blocks + 3]),
         pltpu.make_async_copy(listed_ref, lv, in_sems.at[blocks]),
         pltpu.make_async_copy(flips_ref, fv, in_sems.at[blocks + 1]),
         pltpu.make_async_copy(targets_ref, tv, in_sems.at[blocks + 2]),
     )
     small[0].start()
     small[1].start()
+    small[2].start()
     chunk_copy(0).start()
-    small[2].start()
+    small[3].start()
     for b in range(1, blocks):
         chunk_copy(b).start()
 
     barrier = pltpu.get_barrier_semaphore()
-
-    @pl.loop(1, 64)
-    def _(k):
-        pl.semaphore_signal(
-            barrier, inc=1, device_id=((row + k) % 64, col), device_id_type=MESH
-        )
 
     def z_peer(k):
         other = (z + k) % 8
@@ -105,6 +196,7 @@
             pl.semaphore_signal(barrier, inc=1, device_id=z_peer(k), device_id_type=MESH)
 
     small[0].wait()
+    small[1].wait()
     picked = lv[:, pl.ds(pl.multiple_of(col * picks, picks), picks)]
     eye = lax.broadcasted_iota(jnp.int32, (picks, picks), 0) == lax.broadcasted_iota(
         jnp.int32, (picks, picks), 1
@@ -114,7 +206,7 @@
         target_block = line // block_len
         source = jnp.zeros_like(line)
         for b in range(blocks):
-            source = jnp.where(target_block == b, order_ref[t, b], source)
+            source = jnp.where(target_block == b, order[t, b], source)
         code = (source * block_len + line % block_len).astype(F32)
         column = jnp.sum(
             jnp.where(eye, jnp.broadcast_to(code, (picks, picks)), 0.0), axis=1, keepdims=True
@@ -131,31 +223,33 @@
             walsh[t * picks : (t + 1) * picks, h * 128 : (h + 1) * 128] = (
                 (1 - 2 * bits).astype(F32).astype(BF16)
             )
-    small[1].wait()
     small[2].wait()
+    width = 2 * block_len
     acc[...] = jnp.zeros_like(acc)
-
-    def block_terms(b, lhs):
-        lanes = pl.ds(pl.multiple_of(b * block_len, block_len), block_len)
-        pltpu.make_async_copy(
-            design_ref.at[:, lanes], dv.at[:, lanes], in_sems.at[b]
-        ).wait()
-        for t in range(steps):
-            own = slice(t * picks, (t + 1) * picks)
-            sign = (2 * fv[t : t + 1, lanes] - 1).astype(F32).astype(BF16)
-            chosen = jnp.where(srcs[own, 0:128] == b, 1.0, 0.0).astype(BF16)
-            for h in range(block_len // 128):
-                part = slice(h * 128, (h + 1) * 128)
-                lhs[own, part] = walsh[own, part] * chosen * sign[:, part]
-        first = steps * picks
-        lhs[first : first + 64, :] = dv[pl.ds(pl.multiple_of(col * 64, 64), 64), lanes]
-        lhs[first + 64 : first + 96, :] = tv[:, lanes]
-        acc[...] += lax.dot_general(lhs[...], dv[:, lanes], NT, preferred_element_type=F32)
 
     @pl.loop(0, blocks // 2)
     def _(pair):
-        block_terms(2 * pair, lhs_a)
-        block_terms(2 * pair + 1, lhs_b)
+        @pl.when(pair < 7)
+        def _():
+            for k in range(9):
+                peer = (row + pair * 9 + k + 1) % 64
+                pl.semaphore_signal(barrier, inc=1, device_id=(peer, col), device_id_type=MESH)
+
+        lanes = pl.ds(pl.multiple_of(pair * width, width), width)
+        for b in range(2):
+            here = pl.ds(pl.multiple_of(pair * width, width) + b * block_len, block_len)
+            pltpu.make_async_copy(
+                design_ref.at[:, here], dv.at[:, here], in_sems.at[2 * pair + b]
+            ).wait()
+            for t in range(steps):
+                own = slice(t * picks, (t + 1) * picks)
+                sign = (2 * fv[t : t + 1, here] - 1).astype(F32).astype(BF16)
+                chosen = jnp.where(srcs[own, :] == 2 * pair + b, 1.0, 0.0).astype(BF16)
+                for h in range(block_len // 128):
+                    part = slice(h * 128, (h + 1) * 128)
+                    place = slice(b * block_len + h * 128, b * block_len + (h + 1) * 128)
+                    lhs[own, place] = walsh[own, part] * chosen * sign[:, part]
+        acc[...] += lax.dot_general(lhs[...], dv[:, lanes], NT, preferred_element_type=F32)
 
     for half in range(2):
         lanes = slice(half * 128, (half + 1) * 128)
@@ -164,13 +258,6 @@
                 first = t * picks + rb * 8
                 tile = (acc[first : first + 8, lanes] * inv_root).astype(BF16)
                 xs[2 * (half * 16 + rb) + t] = tile.astype(F32) * keep_scale
-            first = 2 * picks + rb * 4
-            xe[2 * (half * 16 + rb) + 1] = acc[first : first + 4, lanes]
-            if rb < 8:
-                first = 2 * picks + 64 + rb * 4
-                xe[2 * (half * 16 + rb)] = acc[first : first + 4, lanes]
-            else:
-                xe[2 * (half * 16 + rb)] = jnp.zeros((4, 128), F32)
 
     pl.semaphore_wait(barrier, 63 + 6)
 
@@ -215,6 +302,25 @@
         return (sums[0] + sums[1]) + (sums[2] + sums[3])
 
     scatter(xs, rs_s, 0)
+
+    small[3].wait()
+    acc_e[...] = jnp.zeros_like(acc_e)
+
+    @pl.loop(0, blocks // 4)
+    def _(part):
+        lanes = pl.ds(pl.multiple_of(part * 2 * width, 2 * width), 2 * width)
+        own = dv[pl.ds(pl.multiple_of(col * 64, 64), 64), lanes]
+        both = jnp.concatenate([own, tv[:, lanes]], axis=0)
+        acc_e[...] += lax.dot_general(both, dv[:, lanes], NT, preferred_element_type=F32)
+
+    for half in range(2):
+        lanes = slice(half * 128, (half + 1) * 128)
+        for rb in range(16):
+            xe[2 * (half * 16 + rb) + 1] = acc_e[rb * 4 : rb * 4 + 4, lanes]
+            if rb < 8:
+                xe[2 * (half * 16 + rb)] = acc_e[64 + rb * 4 : 68 + rb * 4, lanes]
+            else:
+                xe[2 * (half * 16 + rb)] = jnp.zeros((4, 128), F32)
     scatter(xe, rs_e, 1)
     all_of(rs_s, 0).wait_recv()
     sf[z, xy] = total(xs[row], rs_s)
@@ -248,31 +354,7 @@
     )
     mat[...] = gram + jnp.where(diagonal, shift, 0.0)
 
-    lane_ids = lax.broadcasted_iota(jnp.int32, (NB, unknowns), 1)
-    row_ids = lax.broadcasted_iota(jnp.int32, (NB, unknowns), 0)
-    for k0 in range(0, unknowns, NB):
-        band = slice(k0, k0 + NB)
-        panel = mat[band, :]
-        signed = jnp.where(lane_ids < k0, -panel, panel)
-        left_hi, left_lo = split(signed)
-        left = jnp.concatenate([left_hi, left_hi, left_lo], axis=0)
-        for j in range(NB):
-            c = k0 + j
-            column = panel[:, c : c + 1]
-            inverse = 1.0 / panel[j : j + 1, c : c + 1]
-            cleared = jnp.where(lane_ids == c, 0.0, panel)
-            line = jnp.where(lane_ids[0:1] == c, 1.0, panel[j : j + 1, :]) * inverse
-            panel = jnp.where(row_ids == j, line, cleared - column * line)
-        right_hi, right_lo = split(panel)
-        right = jnp.concatenate([right_hi, right_lo, right_hi], axis=0)
-        update = lax.dot_general(left, right, TN, preferred_element_type=F32)
-        for other in range(0, unknowns, NB):
-            here = slice(other, other + NB)
-            if other == k0:
-                mat[here, :] = panel
-            else:
-                kept = jnp.where((lane_ids >= k0) & (lane_ids < k0 + NB), 0.0, mat[here, :])
-                mat[here, :] = kept - update[here, :]
+    invert(mat)
 
     all_of(ef.at[:, 0:15], 5).wait_recv()
 
@@ -321,22 +403,26 @@
     unknowns, rows_here = design.shape
     block_len = rows_here // block_order.shape[2]
     rhs = targets.shape[0]
-    any_space = pl.BlockSpec(memory_space=pl.ANY)
-    solved = pl.pallas_call(
+    order = block_order.reshape(2, block_order.shape[2])
+    given = (order, design, targets, flip_bits, listed)
+    solved, near_design, near_targets = pl.pallas_call(
         kernel,
-        out_shape=jax.ShapeDtypeStruct((rhs, unknowns), F32),
-        in_specs=[pl.BlockSpec(memory_space=pltpu.SMEM)] + [any_space] * 4,
-        out_specs=pl.BlockSpec(memory_space=pltpu.VMEM),
+        out_shape=(
+            jax.ShapeDtypeStruct((rhs, unknowns), F32),
+            jax.ShapeDtypeStruct(design.shape, BF16),
+            jax.ShapeDtypeStruct(targets.shape, BF16),
+        ),
+        in_specs=[pl.BlockSpec(memory_space=pltpu.HBM)] * 5,
+        out_specs=[pl.BlockSpec(memory_space=pltpu.VMEM)] * 3,
         scratch_shapes=[
-            pltpu.VMEM((unknowns, rows_here), BF16),
-            pltpu.VMEM((rhs, rows_here), BF16),
+            pltpu.SMEM((2, block_order.shape[2]), jnp.int32),
             pltpu.VMEM((2, rows_here), jnp.int32),
             pltpu.VMEM((2, 512), jnp.int32),
             pltpu.VMEM((256, block_len), BF16),
             pltpu.VMEM((256, 128), jnp.int32),
-            pltpu.VMEM((352, block_len), BF16),
-            pltpu.VMEM((352, block_len), BF16),
-            pltpu.VMEM((352, unknowns), F32),
+            pltpu.VMEM((256, 2 * block_len), BF16),
+            pltpu.VMEM((256, unknowns), F32),
+            pltpu.VMEM((96, unknowns), F32),
             pltpu.VMEM((64, 8, 128), F32),
             pltpu.VMEM((64, 4, 128), F32),
             pltpu.VMEM((63, 8, 128), F32),
@@ -350,7 +436,7 @@
             pltpu.VMEM((2 * rhs, unknowns), F32),
             pltpu.VMEM((rhs, unknowns), F32),
             pltpu.VMEM((rhs, unknowns), F32),
-            pltpu.SemaphoreType.DMA((block_order.shape[2] + 3,)),
+            pltpu.SemaphoreType.DMA((block_order.shape[2] + 4,)),
             pltpu.SemaphoreType.DMA((8,)),
             pltpu.SemaphoreType.DMA((8,)),
         ],
@@ -358,10 +444,10 @@
             collective_id=0, has_side_effects=True, vmem_limit_bytes=40 * 1024 * 1024
         ),
         name="sketch_solve",
-    )(block_order.reshape(2, block_order.shape[2]), design, targets, flip_bits, listed)
+    )(*(pltpu.with_memory_space_constraint(v, pltpu.HBM) for v in given))
     residual = jnp.dot(
-        solved.astype(BF16), design, preferred_element_type=F32
-    ) - targets.astype(F32)
+        solved.astype(BF16), near_design, preferred_element_type=F32
+    ) - near_targets.astype(F32)
     return (solved.T, residual)
 
 

time: 78.8 us -> 52.9 us (0.67)
  Pallas kernels: 67.6 us -> 48.7 us
  local copies, waits for them, and re-layouts: 7.48 us -> 0.61 us
    pallas_call x1, Pallas kernels: 67.6 us -> 48.7 us  [on_device(): pl.pallas_call(kernel, out_shape=(jax.ShapeDtypeStruct((rhs, unknowns), F...]
    unnamed x11 -> x1, local copies, waits for them, and re-layouts: 7.48 us -> 0.61 us
where the time goes in v2:
time: 52.9 us; the launch traced here: 52.8 us
  Pallas kernels  48.7 us (92%)
  matrix products  2.87 us (5%)
  between operations  0.64 us (1%)
  local copies, waits for them, and re-layouts  0.61 us (1%)
    pallas_call x1, Pallas kernels, on_device(): pl.pallas_call(kernel, out_shape=(jax.ShapeDtypeStruct((rhs, unknowns), F...  48.7 us
    dot_general x1, matrix products, on_device(): jnp.dot(solved.astype(BF16), near_design, preferred_element_type=F32)  2.87 us

profile of v2, /device:TPU:1, one launch (start us, length us, event | category | flops | bytes accessed | tf_op | source)
XLA Modules:
  0.0 52.8 jit_solution(7576521483636348194)
XLA Ops:
  0.6 48.7 %sketch_solve.1 = (f32[32,256]{1,0:T(8,128)S(1)}, bf16[256,16384]{1,0:T(8,128)(2,1)S(1)}, bf16[32,16384]{1,0:T(8,128)(2,1)S(1)}) custom-call(s32[2,16]{1,0:T(2,128)} %bitcast.4, bf16[256,16384]{1,0:T(8,128)(2,1)} %design_ref.1, bf16[32,16384]{1,0:T(8,128)(2,1)} %targets_ref.1, s32[2,16384]{1,0:T(2,128)} %flips_ref.1, s32[2,512]{1,0:T(2,128)} %listed_ref.1), custom_call_target="tpu_custom_call" | custom-call | tf_op jit(solution)/shard_map/sketch_solve/pallas_call | solution.py:408
  49.3 2.9 %convolution_subtract_fusion = f32[32,16384]{1,0:T(8,128)} fusion(bf16[256,16384]{1,0:T(8,128)(2,1)S(1)} %get-tuple-element.6, bf16[32,16384]{1,0:T(8,128)(2,1)S(1)} %get-tuple-element.7, f32[32,256]{1,0:T(8,128)S(1)} %get-tuple-element.5), kind=kOutput, calls=%fused_computation | convolution fusion | flops 269492224 | bytes 11567104 | tf_op jit(solution)/shard_map/dot_general | solution.py:448
  52.2 0.6 %copy.8 = f32[256,32]{0,1:T(8,128)} copy(f32[256,32]{0,1:T(8,128)S(1)} %bitcast.3) | data formatting | bytes 65536

commit v3 on v2

--- a/solution.py
+++ b/solution.py
@@ -17,6 +17,13 @@
 HIGHEST = lax.Precision.HIGHEST
 
 
+def parity_sign(bits):
+    bits = bits ^ (bits >> 4)
+    bits = bits ^ (bits >> 2)
+    bits = (bits ^ (bits >> 1)) & 1
+    return (1 - 2 * bits).astype(F32)
+
+
 def split(x):
     hi = x.astype(BF16)
     return hi, (x - hi.astype(F32)).astype(BF16)
@@ -41,20 +48,18 @@
     for q in range(0, 8, 2):
         a, b, c = row_of(cols[q], q), row_of(cols[q + 1], q), row_of(cols[q + 1], q + 1)
         r = 1.0 / (a * c - b * b)
-        p00, p01, p11 = c * r, -b * r, a * r
-        w0 = -(cols[q] * p00 + cols[q + 1] * p01)
-        w1 = -(cols[q] * p01 + cols[q + 1] * p11)
-        w0 = jnp.where(sub == q, p00, jnp.where(sub == q + 1, p01, w0))
-        w1 = jnp.where(sub == q, p01, jnp.where(sub == q + 1, p11, w1))
+        t0, t1 = cols[q] * c - cols[q + 1] * b, cols[q + 1] * a - cols[q] * b
+        t0 = jnp.where(sub == q, -c, jnp.where(sub == q + 1, b, t0))
+        t1 = jnp.where(sub == q, b, jnp.where(sub == q + 1, -a, t1))
         fresh = []
         for j in range(8):
             if j == q:
-                fresh.append(w0)
+                fresh.append(-(r * t0))
             elif j == q + 1:
-                fresh.append(w1)
+                fresh.append(-(r * t1))
             else:
                 kept = jnp.where((sub == q) | (sub == q + 1), 0.0, cols[j])
-                fresh.append(kept + (w0 * row_of(cols[j], q) + w1 * row_of(cols[j], q + 1)))
+                fresh.append(kept - r * (t0 * row_of(cols[j], q) + t1 * row_of(cols[j], q + 1)))
         cols = fresh
     return cols
 
@@ -62,30 +67,43 @@
 def eliminate(tiles, k0, sub, lane):
     home = k0 // 128
     groups = NB // 8
+    ahead = None
     for s in range(groups):
         c0 = k0 + 8 * s - 128 * home
-        cols = [[lane_of(tiles[g][home], c0 + j) for g in range(groups)] for j in range(8)]
-        inverse = small_inverse([cols[j][s] for j in range(8)], sub)
+        diagonal = ahead or [lane_of(tiles[s][home], c0 + j) for j in range(8)]
+        inverse = small_inverse(diagonal, sub)
+        if s + 1 < groups:
+            low = [lane_of(tiles[s + 1][home], c0 + j) for j in range(8)]
+            after = [lane_of(tiles[s + 1][home], c0 + 8 + j) for j in range(8)]
+            scaled = [
+                tree([low[i] * row_of(inverse[j], i) for i in range(8)]) for j in range(8)
+            ]
+            ahead = [
+                after[j] - tree([scaled[i] * row_of(low[i], j) for i in range(8)])
+                for j in range(8)
+            ]
+        cols = [
+            [diagonal[j] if g == s else lane_of(tiles[g][home], c0 + j) for g in range(groups)]
+            for j in range(8)
+        ]
         inside = (lane >= c0) & (lane < c0 + 8)
         unit = jnp.where(lane == sub + c0, 1.0, 0.0)
         lead = [jnp.where(inside, unit, t) if h == home else t for h, t in enumerate(tiles[s])]
         fresh = [tree([inverse[j] * row_of(lead[h], j) for j in range(8)]) for h in range(2)]
         rows = [[row_of(fresh[h], j) for j in range(8)] for h in range(2)]
-        after = []
-        for g in range(groups):
-            if g == s:
-                after.append(fresh)
-                continue
-            line = []
-            for h in range(2):
+        moved = [None] * groups
+        moved[s] = fresh
+        for g in [(s + d) % groups for d in range(1, groups)]:
+            line = [None, None]
+            for h in (home, 1 - home):
                 kept = jnp.where(inside, 0.0, tiles[g][h]) if h == home else tiles[g][h]
-                line.append(kept - tree([cols[j][g] * rows[h][j] for j in range(8)]))
-            after.append(line)
-        tiles = after
+                line[h] = kept - tree([cols[j][g] * rows[h][j] for j in range(8)])
+            moved[g] = line
+        tiles = moved
     return tiles
 
 
-def invert(mat):
+def invert(mat, after_round):
     n = mat.shape[0]
     sub = lax.broadcasted_iota(jnp.int32, (8, 128), 0)
     lane = lax.broadcasted_iota(jnp.int32, (8, 128), 1)
@@ -114,6 +132,7 @@
                 mat[here, :] = done
             elif other != k1:
                 mat[here, :] = jnp.where(inside, 0.0, mat[here, :]) - update[here, :]
+        after_round(k0 // NB)
 
 
 def kernel(
@@ -130,7 +149,8 @@
     lv,
     walsh,
     srcs,
-    lhs,
+    lhs_a,
+    lhs_b,
     acc,
     acc_e,
     xs,
@@ -142,6 +162,7 @@
     mat,
     gmat,
     bt,
+    b_near,
     xsend,
     xrecv,
     ysend,
@@ -189,6 +210,9 @@
         other = (z + k) % 8
         return ((other % 2) * 32 + row % 32, other // 2)
 
+    for mask in range(1, 64):
+        pl.semaphore_signal(barrier, inc=1, device_id=(row ^ mask, col), device_id_type=MESH)
+
     for k in range(1, 8):
 
         @pl.when(((z + k) % 8) // 2 != col)
@@ -213,34 +237,19 @@
         ).astype(jnp.int32)
         srcs[t * picks : (t + 1) * picks, :] = jnp.broadcast_to(column // block_len, (picks, 128))
         within = column % block_len
+        low = parity_sign(within & lax.broadcasted_iota(jnp.int32, (picks, 128), 1)).astype(BF16)
+        high = jnp.broadcast_to(within // 128, (picks, 128))
         for h in range(block_len // 128):
-            places = lax.broadcasted_iota(jnp.int32, (picks, 128), 1) + h * 128
-            bits = within & places
-            bits = bits ^ (bits >> 8)
-            bits = bits ^ (bits >> 4)
-            bits = bits ^ (bits >> 2)
-            bits = (bits ^ (bits >> 1)) & 1
-            walsh[t * picks : (t + 1) * picks, h * 128 : (h + 1) * 128] = (
-                (1 - 2 * bits).astype(F32).astype(BF16)
-            )
+            walsh[t * picks : (t + 1) * picks, h * 128 : (h + 1) * 128] = low * parity_sign(
+                high & h
+            ).astype(BF16)
     small[2].wait()
     width = 2 * block_len
     acc[...] = jnp.zeros_like(acc)
 
-    @pl.loop(0, blocks // 2)
-    def _(pair):
-        @pl.when(pair < 7)
-        def _():
-            for k in range(9):
-                peer = (row + pair * 9 + k + 1) % 64
-                pl.semaphore_signal(barrier, inc=1, device_id=(peer, col), device_id_type=MESH)
-
-        lanes = pl.ds(pl.multiple_of(pair * width, width), width)
+    def build(pair, lhs):
         for b in range(2):
             here = pl.ds(pl.multiple_of(pair * width, width) + b * block_len, block_len)
-            pltpu.make_async_copy(
-                design_ref.at[:, here], dv.at[:, here], in_sems.at[2 * pair + b]
-            ).wait()
             for t in range(steps):
                 own = slice(t * picks, (t + 1) * picks)
                 sign = (2 * fv[t : t + 1, here] - 1).astype(F32).astype(BF16)
@@ -249,7 +258,28 @@
                     part = slice(h * 128, (h + 1) * 128)
                     place = slice(b * block_len + h * 128, b * block_len + (h + 1) * 128)
                     lhs[own, place] = walsh[own, part] * chosen * sign[:, part]
+
+    def apply(pair, lhs):
+        lanes = pl.ds(pl.multiple_of(pair * width, width), width)
         acc[...] += lax.dot_general(lhs[...], dv[:, lanes], NT, preferred_element_type=F32)
+
+    def arrived(pair):
+        for b in range(2):
+            here = pl.ds(pl.multiple_of(pair * width, width) + b * block_len, block_len)
+            pltpu.make_async_copy(
+                design_ref.at[:, here], dv.at[:, here], in_sems.at[2 * pair + b]
+            ).wait()
+
+    build(0, lhs_a)
+
+    @pl.loop(0, blocks // 4)
+    def _(quad):
+        arrived(2 * quad)
+        arrived(2 * quad + 1)
+        build(2 * quad + 1, lhs_b)
+        apply(2 * quad, lhs_a)
+        build(jnp.minimum(2 * quad + 2, blocks // 2 - 1), lhs_a)
+        apply(2 * quad + 1, lhs_b)
 
     for half in range(2):
         lanes = slice(half * 128, (half + 1) * 128)
@@ -271,23 +301,26 @@
             device_id_type=MESH,
         )
 
+    def hops(mask):
+        ring = (0, 1, 2, 1)
+        return (mask >> 5) + ring[mask >> 3 & 3] + ring[mask >> 1 & 3]
+
     def scatter(src, dst, stage):
-        @pl.loop(1, 64)
-        def _(k):
-            peer = (row + k) % 64
-            remote(src.at[peer], dst.at[k - 1], stage, (peer, col)).start()
+        for mask in sorted(range(1, 64), key=lambda m: (-hops(m), m)):
+            peer = row ^ mask
+            remote(src.at[peer], dst.at[mask - 1], stage, (peer, col)).start()
+
+    plane = sorted(range(1, 16), key=lambda m: (-hops(2 * m), m))
 
     def gather_z(full, stage):
-        @pl.loop(1, 8)
-        def _(k):
+        for k in (4, 3, 5, 2, 6, 1, 7):
             place = full.at[z, xy]
             remote(place, place, stage, z_peer(k)).start()
 
     def gather_xy(full, stage):
-        @pl.loop(1, 16)
-        def _(k):
+        for mask in plane:
             place = full.at[:, xy]
-            peer = z_lo * 32 + ((xy + k) % 16) * 2 + core
+            peer = row ^ (2 * mask)
             remote(place, place, stage, (peer, col)).start()
 
     def all_of(buffer, stage):
@@ -324,14 +357,20 @@
     scatter(xe, rs_e, 1)
     all_of(rs_s, 0).wait_recv()
     sf[z, xy] = total(xs[row], rs_s)
-    gather_z(sf, 2)
+    near_first = (1, 7, 2, 6, 3, 5, 4)
+    for k in reversed(near_first):
+        place = sf.at[z, xy]
+        remote(place, place, 7 + k, z_peer(k)).start()
+    for k in (0,) + near_first:
+        place = sf.at[(z + 8 - k) % 8, xy]
+        if k:
+            remote(place, place, 7 + k, z_peer(k)).wait_recv()
+        for mask in plane:
+            remote(place, place, 4, (row ^ (2 * mask), col)).start()
+
     all_of(rs_e, 1).wait_recv()
     ef[z, xy] = total(xe[row], rs_e)
     gather_z(ef, 3)
-    all_of(rs_s.at[0:7], 2).wait_recv()
-    gather_xy(sf, 4)
-    all_of(rs_e.at[0:7], 3).wait_recv()
-    gather_xy(ef, 5)
     all_of(sf.at[:, 0:15], 4).wait_recv()
 
     squares = jnp.zeros((8, 128), F32)
@@ -352,39 +391,59 @@
     diagonal = lax.broadcasted_iota(jnp.int32, (unknowns, unknowns), 0) == lax.broadcasted_iota(
         jnp.int32, (unknowns, unknowns), 1
     )
-    mat[...] = gram + jnp.where(diagonal, shift, 0.0)
-
-    invert(mat)
-
-    all_of(ef.at[:, 0:15], 5).wait_recv()
+    unscale = 1.0 / shift
+    mat[...] = gram * unscale + jnp.where(diagonal, 1.0, 0.0)
+
+    def after_round(done):
+        if done == 0:
+            all_of(rs_e.at[0:7], 3).wait_recv()
+            gather_xy(ef, 5)
+        if done == 6:
+            all_of(ef.at[:, 0:15], 5).wait_recv()
+            for half in range(2):
+                lanes = slice(half * 128, (half + 1) * 128)
+                for rb in range(8):
+                    bt[rb * 4 : rb * 4 + 4, lanes] = ef[2 * col + half, rb]
+                for c in range(4):
+                    for rb in range(16):
+                        first = c * 64 + rb * 4
+                        gmat[first : first + 4, lanes] = ef[2 * c + half, rb]
+
+            @pl.when(core == 0)
+            def _():
+                remote(bt, b_near, 15, (row + 1, col)).start()
+
+    invert(mat, after_round)
+
+    inverse_hi, inverse_lo = split(mat[...] * unscale)
+
+    def times_inverse(value):
+        hi, lo = split(value)
+        out = jnp.dot(hi, inverse_hi, preferred_element_type=F32)
+        out = out + jnp.dot(lo, inverse_hi, preferred_element_type=F32)
+        return out + jnp.dot(hi, inverse_lo, preferred_element_type=F32)
 
     @pl.when(core == 0)
     def _():
-        for half in range(2):
-            for rb in range(8):
-                bt[rb * 4 : rb * 4 + 4, half * 128 : (half + 1) * 128] = ef[2 * col + half, rb]
-        first = jnp.dot(bt[...], mat[...], precision=HIGHEST, preferred_element_type=F32)
-        xsend[0:32, :] = first
-        xsend[32:64, :] = bt[...]
+        xsend[...] = times_inverse(bt[...])
         handed = remote(xsend, xrecv, 6, (row + 1, col))
         handed.start()
         remote(ysend, yrecv, 7, (row + 1, col)).wait_recv()
         out_ref[...] = yrecv[...]
         handed.wait_send()
+        remote(bt, b_near, 15, (row + 1, col)).wait_send()
 
     @pl.when(core == 1)
     def _():
-        for c in range(4):
-            for half in range(2):
-                for rb in range(16):
-                    first = c * 64 + rb * 4
-                    gmat[first : first + 4, half * 128 : (half + 1) * 128] = ef[2 * c + half, rb]
+        remote(bt, b_near, 15, (row - 1, col)).wait_recv()
+        pull = times_inverse(b_near[...])
+        turn_hi, turn_lo = split(times_inverse(gmat[...]))
         remote(xsend, xrecv, 6, (row - 1, col)).wait_recv()
-        start = xrecv[0:32, :]
-        rounded = start.astype(BF16).astype(F32)
-        gradient = jnp.dot(rounded, gmat[...], precision=HIGHEST, preferred_element_type=F32)
-        gradient = gradient - xrecv[32:64, :]
-        moved = start - jnp.dot(gradient, mat[...], precision=HIGHEST, preferred_element_type=F32)
+        start = xrecv[...]
+        rounded = start.astype(BF16)
+        moved = jnp.dot(rounded, turn_hi, preferred_element_type=F32)
+        moved = moved + jnp.dot(rounded, turn_lo, preferred_element_type=F32)
+        moved = start + (pull - moved)
         ysend[...] = moved
         handed = remote(ysend, yrecv, 7, (row - 1, col))
         handed.start()
@@ -393,10 +452,31 @@
 
     all_of(rs_s, 0).wait_send()
     all_of(rs_e, 1).wait_send()
-    all_of(rs_s.at[0:7], 2).wait_send()
+    for k in near_first:
+        remote(rs_s.at[0], rs_s.at[0], 7 + k, z_peer(k)).wait_send()
     all_of(rs_e.at[0:7], 3).wait_send()
     all_of(sf.at[:, 0:15], 4).wait_send()
     all_of(ef.at[:, 0:15], 5).wait_send()
+
+
+def residual_kernel(solved_ref, design_ref, targets_ref, solution_ref, residual_ref, parts, sems):
+    pieces = parts.shape[0]
+    width = parts.shape[2]
+    rounded = solved_ref[...].astype(BF16)
+    solution_copy = pltpu.make_async_copy(solved_ref, solution_ref, sems.at[pieces])
+    solution_copy.start()
+    copies = []
+    for piece in range(pieces):
+        lanes = slice(piece * width, (piece + 1) * width)
+        product = jnp.dot(rounded, design_ref[:, lanes], preferred_element_type=F32)
+        parts[piece] = product - targets_ref[:, lanes].astype(F32)
+        copies.append(
+            pltpu.make_async_copy(parts.at[piece], residual_ref.at[:, lanes], sems.at[piece])
+        )
+        copies[-1].start()
+    for copy in copies:
+        copy.wait()
+    solution_copy.wait()
 
 
 def on_device(design, targets, flip_bits, listed, block_order):
@@ -421,6 +501,7 @@
             pltpu.VMEM((256, block_len), BF16),
             pltpu.VMEM((256, 128), jnp.int32),
             pltpu.VMEM((256, 2 * block_len), BF16),
+            pltpu.VMEM((256, 2 * block_len), BF16),
             pltpu.VMEM((256, unknowns), F32),
             pltpu.VMEM((96, unknowns), F32),
             pltpu.VMEM((64, 8, 128), F32),
@@ -432,23 +513,36 @@
             pltpu.VMEM((unknowns, unknowns), F32),
             pltpu.VMEM((unknowns, unknowns), F32),
             pltpu.VMEM((rhs, unknowns), F32),
-            pltpu.VMEM((2 * rhs, unknowns), F32),
-            pltpu.VMEM((2 * rhs, unknowns), F32),
+            pltpu.VMEM((rhs, unknowns), F32),
+            pltpu.VMEM((rhs, unknowns), F32),
+            pltpu.VMEM((rhs, unknowns), F32),
             pltpu.VMEM((rhs, unknowns), F32),
             pltpu.VMEM((rhs, unknowns), F32),
             pltpu.SemaphoreType.DMA((block_order.shape[2] + 4,)),
-            pltpu.SemaphoreType.DMA((8,)),
-            pltpu.SemaphoreType.DMA((8,)),
+            pltpu.SemaphoreType.DMA((16,)),
+            pltpu.SemaphoreType.DMA((16,)),
         ],
         compiler_params=pltpu.CompilerParams(
             collective_id=0, has_side_effects=True, vmem_limit_bytes=40 * 1024 * 1024
         ),
         name="sketch_solve",
     )(*(pltpu.with_memory_space_constraint(v, pltpu.HBM) for v in given))
-    residual = jnp.dot(
-        solved.astype(BF16), near_design, preferred_element_type=F32
-    ) - near_targets.astype(F32)
-    return (solved.T, residual)
+    out, residual = pl.pallas_call(
+        residual_kernel,
+        out_shape=(
+            jax.ShapeDtypeStruct((rhs, unknowns), F32),
+            jax.ShapeDtypeStruct(targets.shape, F32),
+        ),
+        in_specs=[pl.BlockSpec(memory_space=pltpu.VMEM)] * 3,
+        out_specs=[pl.BlockSpec(memory_space=pltpu.HBM)] * 2,
+        scratch_shapes=[
+            pltpu.VMEM((8, rhs, rows_here // 8), F32),
+            pltpu.SemaphoreType.DMA((9,)),
+        ],
+        compiler_params=pltpu.CompilerParams(vmem_limit_bytes=16 * 1024 * 1024),
+        name="residual",
+    )(solved, near_design, near_targets)
+    return (out.T, residual)
 
 
 def solution(mesh):

time: 52.9 us -> 45.7 us (0.86)
  Pallas kernels: 48.7 us -> 45 us
  matrix products: 2.87 us -> 0 us
  local copies, waits for them, and re-layouts: 0.61 us -> 0 us
    pallas_call x1, Pallas kernels: 48.7 us -> 42.6 us  [on_device(): pl.pallas_call(kernel, out_shape=(jax.ShapeDtypeStruct((rhs, unknowns), F...]
    dot_general x1 -> x0, matrix products: 2.87 us -> none  [on_device(): jnp.dot(solved.astype(BF16), near_design, preferred_element_type=F32)]
    pallas_call x0 -> x1, Pallas kernels: none -> 2.35 us  [on_device(): pl.pallas_call(residual_kernel, out_shape=(jax.ShapeDtypeStruct((rhs, unk...]
    unnamed x1 -> x0, local copies, waits for them, and re-layouts: 0.61 us -> none
where the time goes in v3:
time: 45.7 us; the launch traced here: 45.6 us
  Pallas kernels  45 us (98%)
  between operations  0.64 us (1%)
    pallas_call x1, Pallas kernels, on_device(): pl.pallas_call(kernel, out_shape=(jax.ShapeDtypeStruct((rhs, unknowns), F...  42.6 us
    pallas_call x1, Pallas kernels, on_device(): pl.pallas_call(residual_kernel, out_shape=(jax.ShapeDtypeStruct((rhs, unk...  2.35 us

profile of v3, /device:TPU:1, one launch (start us, length us, event | category | flops | bytes accessed | tf_op | source)
XLA Modules:
  0.0 45.6 jit_solution(10306883407117944325)
XLA Ops:
  0.6 42.6 %sketch_solve.1 = (f32[32,256]{1,0:T(8,128)S(1)}, bf16[256,16384]{1,0:T(8,128)(2,1)S(1)}, bf16[32,16384]{1,0:T(8,128)(2,1)S(1)}) custom-call(s32[2,16]{1,0:T(2,128)} %bitcast.2, bf16[256,16384]{1,0:T(8,128)(2,1)} %design_ref.1, bf16[32,16384]{1,0:T(8,128)(2,1)} %targets_ref.1, s32[2,16384]{1,0:T(2,128)} %flips_ref.1, s32[2,512]{1,0:T(2,128)} %listed_ref.1), custom_call_target="tpu_custom_call" | custom-call | tf_op jit(solution)/shard_map/sketch_solve/pallas_call | solution.py:488
  43.3 2.4 %residual.1 = (f32[32,256]{1,0:T(8,128)}, f32[32,16384]{1,0:T(8,128)}) custom-call(f32[32,256]{1,0:T(8,128)S(1)} %get-tuple-element.7.solved_ref, bf16[256,16384]{1,0:T(8,128)(2,1)S(1)} %get-tuple-element.8.design_ref, bf16[32,16384]{1,0:T(8,128)(2,1)S(1)} %get-tuple-element.9.targets_ref), custom_call_target="tpu_custom_call" | custom-call | tf_op jit(solution)/shard_map/residual/pallas_call | solution.py:530

commit v4 on v3

--- a/solution.py
+++ b/solution.py
@@ -11,9 +11,10 @@
 MESH = pl.DeviceIdType.MESH
 F32 = jnp.float32
 BF16 = jnp.bfloat16
-NB = 32
+NB = 16
 NT = (((1,), (1,)), ((), ()))
 TN = (((0,), (0,)), ((), ()))
+NN = (((1,), (0,)), ((), ()))
 HIGHEST = lax.Precision.HIGHEST
 
 
@@ -22,6 +23,13 @@
     bits = bits ^ (bits >> 2)
     bits = (bits ^ (bits >> 1)) & 1
     return (1 - 2 * bits).astype(F32)
+
+
+def product(a, b, dims):
+    (a_hi, a_lo), (b_hi, b_lo) = split(a), split(b)
+    out = lax.dot_general(a_hi, b_hi, dims, preferred_element_type=F32)
+    out = out + lax.dot_general(a_hi, b_lo, dims, preferred_element_type=F32)
+    return out + lax.dot_general(a_lo, b_hi, dims, preferred_element_type=F32)
 
 
 def split(x):
@@ -89,15 +97,15 @@
         inside = (lane >= c0) & (lane < c0 + 8)
         unit = jnp.where(lane == sub + c0, 1.0, 0.0)
         lead = [jnp.where(inside, unit, t) if h == home else t for h, t in enumerate(tiles[s])]
-        fresh = [tree([inverse[j] * row_of(lead[h], j) for j in range(8)]) for h in range(2)]
-        rows = [[row_of(fresh[h], j) for j in range(8)] for h in range(2)]
+        fresh = [tree([inverse[j] * row_of(t, j) for j in range(8)]) for t in lead]
+        rows = [[row_of(t, j) for j in range(8)] for t in fresh]
         moved = [None] * groups
         moved[s] = fresh
         for g in [(s + d) % groups for d in range(1, groups)]:
-            line = [None, None]
-            for h in (home, 1 - home):
-                kept = jnp.where(inside, 0.0, tiles[g][h]) if h == home else tiles[g][h]
-                line[h] = kept - tree([cols[j][g] * rows[h][j] for j in range(8)])
+            line = []
+            for h, tile in enumerate(tiles[g]):
+                kept = jnp.where(inside, 0.0, tile) if h == home else tile
+                line.append(kept - tree([cols[j][g] * rows[h][j] for j in range(8)]))
             moved[g] = line
         tiles = moved
     return tiles
@@ -114,7 +122,7 @@
         left_hi, left_lo = split(jnp.where(wide < k0, -panel, panel))
         left = jnp.concatenate([left_hi, left_hi, left_lo], axis=0)
         tiles = [
-            [panel[8 * g : 8 * g + 8, 128 * h : 128 * h + 128] for h in range(2)]
+            [panel[8 * g : 8 * g + 8, lane0 : lane0 + 128] for lane0 in range(0, n, 128)]
             for g in range(NB // 8)
         ]
         tiles = eliminate(tiles, k0, sub, lane)
@@ -162,11 +170,12 @@
     mat,
     gmat,
     bt,
-    b_near,
-    xsend,
-    xrecv,
-    ysend,
-    yrecv,
+    start_at,
+    last,
+    top,
+    tail,
+    ratio_ref,
+    sums,
     in_sems,
     send_sems,
     recv_sems,
@@ -327,12 +336,10 @@
         return remote(buffer, buffer, stage, (row, col))
 
     def total(own, parts):
-        sums = [own]
-        for lead in range(3):
-            sums.append(parts[lead])
+        lines = [own] + [parts[lead] for lead in range(3)]
         for index in range(3, 63):
-            sums[index % 4] = sums[index % 4] + parts[index]
-        return (sums[0] + sums[1]) + (sums[2] + sums[3])
+            lines[index % 4] = lines[index % 4] + parts[index]
+        return (lines[0] + lines[1]) + (lines[2] + lines[3])
 
     scatter(xs, rs_s, 0)
 
@@ -357,105 +364,149 @@
     scatter(xe, rs_e, 1)
     all_of(rs_s, 0).wait_recv()
     sf[z, xy] = total(xs[row], rs_s)
-    near_first = (1, 7, 2, 6, 3, 5, 4)
-    for k in reversed(near_first):
+    for k in (4, 3, 5, 2, 6, 1, 7):
         place = sf.at[z, xy]
         remote(place, place, 7 + k, z_peer(k)).start()
-    for k in (0,) + near_first:
+
+    def along_z(k):
         place = sf.at[(z + 8 - k) % 8, xy]
         if k:
             remote(place, place, 7 + k, z_peer(k)).wait_recv()
+
+    def over_plane(k, stage):
+        place = sf.at[(z + 8 - k) % 8, xy]
         for mask in plane:
-            remote(place, place, 4, (row ^ (2 * mask), col)).start()
-
+            remote(place, place, stage, (row ^ (2 * mask), col)).start()
+
+    even, odd = (0, 2, 6, 4), (1, 7, 3, 5)
+    for parity, first, second in ((0, even, odd), (1, odd, even)):
+
+        @pl.when(z_lo == parity)
+        def _():
+            for k in first:
+                along_z(k)
+                over_plane(k, 4)
+            for k in second:
+                along_z(k)
+
+    sums[xy] = jnp.sum(
+        tree([sf[i, xy] * sf[i, xy] for i in range(8)]), axis=0, keepdims=True
+    )
+    for mask in plane:
+        remote(sums.at[xy], sums.at[xy], 17, (row ^ (2 * mask), col)).start()
+    def send_rest(whose):
+        for parity, second in ((0, odd), (1, even)):
+
+            @pl.when((z_lo == parity) & (core == whose))
+            def _():
+                for k in second:
+                    over_plane(k, 16)
+
+    send_rest(0)
     all_of(rs_e, 1).wait_recv()
     ef[z, xy] = total(xe[row], rs_e)
     gather_z(ef, 3)
-    all_of(sf.at[:, 0:15], 4).wait_recv()
-
-    squares = jnp.zeros((8, 128), F32)
-    halves = []
-    for half in range(2):
-        parts = [sf[2 * c + half].reshape(picks, 128) for c in range(4)]
-        halves.append(jnp.concatenate(parts, axis=0))
-    sketch = jnp.concatenate(halves, axis=1)
-    for first in range(0, 512, 8):
-        for lane in range(0, 256, 128):
-            piece = sketch[first : first + 8, lane : lane + 128]
-            squares = squares + piece * piece
-    hi, lo = split(sketch)
-    gram = lax.dot_general(hi, hi, TN, preferred_element_type=F32)
-    gram = gram + lax.dot_general(hi, lo, TN, preferred_element_type=F32)
-    gram = gram + lax.dot_general(lo, hi, TN, preferred_element_type=F32)
-    shift = jnp.sum(squares) / unknowns
-    diagonal = lax.broadcasted_iota(jnp.int32, (unknowns, unknowns), 0) == lax.broadcasted_iota(
-        jnp.int32, (unknowns, unknowns), 1
-    )
+    all_of(sf.at[0:4, 0:15], 4).wait_recv()
+    all_of(sums.at[0:15], 17).wait_recv()
+    send_rest(1)
+
+    def half_of(half):
+        return jnp.concatenate([sf[2 * c + half].reshape(picks, 128) for c in range(4)], axis=0)
+
+    shift = jnp.sum(tree([sums[i] for i in range(16)])) / unknowns
     unscale = 1.0 / shift
-    mat[...] = gram * unscale + jnp.where(diagonal, 1.0, 0.0)
-
-    def after_round(done):
-        if done == 0:
+    unit = jnp.where(eye, 1.0, 0.0)
+    first_half = half_of(0)
+    top[...] = product(first_half, first_half, TN) * unscale + unit
+
+    def after_top(done):
+        if done == 1:
             all_of(rs_e.at[0:7], 3).wait_recv()
             gather_xy(ef, 5)
-        if done == 6:
+
+    def after_low(done):
+        if done == 5:
             all_of(ef.at[:, 0:15], 5).wait_recv()
-            for half in range(2):
-                lanes = slice(half * 128, (half + 1) * 128)
-                for rb in range(8):
-                    bt[rb * 4 : rb * 4 + 4, lanes] = ef[2 * col + half, rb]
-                for c in range(4):
-                    for rb in range(16):
-                        first = c * 64 + rb * 4
-                        gmat[first : first + 4, lanes] = ef[2 * c + half, rb]
 
             @pl.when(core == 0)
             def _():
-                remote(bt, b_near, 15, (row + 1, col)).start()
-
-    invert(mat, after_round)
-
-    inverse_hi, inverse_lo = split(mat[...] * unscale)
-
-    def times_inverse(value):
-        hi, lo = split(value)
-        out = jnp.dot(hi, inverse_hi, preferred_element_type=F32)
-        out = out + jnp.dot(lo, inverse_hi, preferred_element_type=F32)
-        return out + jnp.dot(hi, inverse_lo, preferred_element_type=F32)
+                for half in range(2):
+                    lanes = slice(half * 128, (half + 1) * 128)
+                    for rb in range(8):
+                        bt[rb * 4 : rb * 4 + 4, lanes] = ef[2 * col + half, rb]
+                remote(bt, bt, 15, (row + 1, col)).start()
+
+            @pl.when(core == 1)
+            def _():
+                for half in range(2):
+                    lanes = slice(half * 128, (half + 1) * 128)
+                    for c in range(4):
+                        for rb in range(16):
+                            first = c * 64 + rb * 4
+                            gmat[first : first + 4, lanes] = ef[2 * c + half, rb]
+                remote(gmat, gmat, 18, (row - 1, col)).start()
+
+    invert(top, after_top)
+    all_of(sf.at[0:4, 0:15], 16).wait_recv()
+    second_half = half_of(1)
+    cross = product(half_of(0), second_half, TN) * unscale
+    ratio = product(top[...], cross, NN)
+    corner = product(second_half, second_half, TN) * unscale + unit
+    tail[...] = corner - product(cross, ratio, TN)
+    ratio_ref[...] = ratio
+    invert(tail, after_low)
+    ratio = ratio_ref[...]
+    corner = tail[...]
+    across = product(ratio, corner, NN)
+    mat[0:128, 0:128] = (top[...] + product(across, ratio, NT)) * unscale
+    mat[0:128, 128:256] = across * -unscale
+    mat[128:256, 0:128] = product(corner, ratio, NT) * -unscale
+    mat[128:256, 128:256] = corner * unscale
 
     @pl.when(core == 0)
     def _():
-        xsend[...] = times_inverse(bt[...])
-        handed = remote(xsend, xrecv, 6, (row + 1, col))
-        handed.start()
-        remote(ysend, yrecv, 7, (row + 1, col)).wait_recv()
-        out_ref[...] = yrecv[...]
-        handed.wait_send()
-        remote(bt, b_near, 15, (row + 1, col)).wait_send()
+        start_at[...] = product(bt[...], mat[...], NN)
+        remote(start_at, start_at, 6, (row + 1, col)).start()
+        remote(gmat, gmat, 18, (row + 1, col)).wait_recv()
 
     @pl.when(core == 1)
     def _():
-        remote(bt, b_near, 15, (row - 1, col)).wait_recv()
-        pull = times_inverse(b_near[...])
-        turn_hi, turn_lo = split(times_inverse(gmat[...]))
-        remote(xsend, xrecv, 6, (row - 1, col)).wait_recv()
-        start = xrecv[...]
-        rounded = start.astype(BF16)
-        moved = jnp.dot(rounded, turn_hi, preferred_element_type=F32)
-        moved = moved + jnp.dot(rounded, turn_lo, preferred_element_type=F32)
-        moved = start + (pull - moved)
-        ysend[...] = moved
-        handed = remote(ysend, yrecv, 7, (row - 1, col))
-        handed.start()
-        out_ref[...] = moved
-        handed.wait_send()
+        last[...] = mat[...]
+        remote(last, last, 7, (row - 1, col)).start()
+        remote(bt, bt, 15, (row - 1, col)).wait_recv()
+        remote(start_at, start_at, 6, (row - 1, col)).wait_recv()
+
+    start = start_at[...]
+    rounded = start.astype(BF16)
+    gram_hi, gram_lo = split(gmat[...])
+    gradient = jnp.dot(rounded, gram_hi, preferred_element_type=F32)
+    gradient = gradient + jnp.dot(rounded, gram_lo, preferred_element_type=F32)
+    gradient = gradient - bt[...]
+
+    @pl.when(core == 0)
+    def _():
+        remote(last, last, 7, (row + 1, col)).wait_recv()
+
+    out_ref[...] = start - product(gradient, last[...], NN)
+
+    @pl.when(core == 0)
+    def _():
+        remote(start_at, start_at, 6, (row + 1, col)).wait_send()
+        remote(bt, bt, 15, (row + 1, col)).wait_send()
+
+    @pl.when(core == 1)
+    def _():
+        remote(last, last, 7, (row - 1, col)).wait_send()
+        remote(gmat, gmat, 18, (row - 1, col)).wait_send()
 
     all_of(rs_s, 0).wait_send()
     all_of(rs_e, 1).wait_send()
-    for k in near_first:
+    for k in range(1, 8):
         remote(rs_s.at[0], rs_s.at[0], 7 + k, z_peer(k)).wait_send()
     all_of(rs_e.at[0:7], 3).wait_send()
-    all_of(sf.at[:, 0:15], 4).wait_send()
+    all_of(sf.at[0:4, 0:15], 4).wait_send()
+    all_of(sf.at[0:4, 0:15], 16).wait_send()
+    all_of(sums.at[0:15], 17).wait_send()
     all_of(ef.at[:, 0:15], 5).wait_send()
 
 
@@ -514,13 +565,14 @@
             pltpu.VMEM((unknowns, unknowns), F32),
             pltpu.VMEM((rhs, unknowns), F32),
             pltpu.VMEM((rhs, unknowns), F32),
-            pltpu.VMEM((rhs, unknowns), F32),
-            pltpu.VMEM((rhs, unknowns), F32),
-            pltpu.VMEM((rhs, unknowns), F32),
-            pltpu.VMEM((rhs, unknowns), F32),
+            pltpu.VMEM((unknowns, unknowns), F32),
+            pltpu.VMEM((128, 128), F32),
+            pltpu.VMEM((128, 128), F32),
+            pltpu.VMEM((128, 128), F32),
+            pltpu.VMEM((16, 1, 128), F32),
             pltpu.SemaphoreType.DMA((block_order.shape[2] + 4,)),
-            pltpu.SemaphoreType.DMA((16,)),
-            pltpu.SemaphoreType.DMA((16,)),
+            pltpu.SemaphoreType.DMA((19,)),
+            pltpu.SemaphoreType.DMA((19,)),
         ],
         compiler_params=pltpu.CompilerParams(
             collective_id=0, has_side_effects=True, vmem_limit_bytes=40 * 1024 * 1024

time: 45.7 us -> 43.1 us (0.943)
  Pallas kernels: 45 us -> 42.4 us
    pallas_call x1, Pallas kernels: 42.6 us -> 40 us  [on_device(): pl.pallas_call(kernel, out_shape=(jax.ShapeDtypeStruct((rhs, unknowns), F...]
where the time goes in v4:
time: 43.1 us; the launch traced here: 43 us
  Pallas kernels  42.4 us (98%)
  between operations  0.64 us (1%)
    pallas_call x1, Pallas kernels, on_device(): pl.pallas_call(kernel, out_shape=(jax.ShapeDtypeStruct((rhs, unknowns), F...  40 us
    pallas_call x1, Pallas kernels, on_device(): pl.pallas_call(residual_kernel, out_shape=(jax.ShapeDtypeStruct((rhs, unk...  2.35 us

profile of v4, /device:TPU:1, one launch (start us, length us, event | category | flops | bytes accessed | tf_op | source)
XLA Modules:
  0.0 43.0 jit_solution(8343236918427611454)
XLA Ops:
  0.6 40.0 %sketch_solve.1 = (f32[32,256]{1,0:T(8,128)S(1)}, bf16[256,16384]{1,0:T(8,128)(2,1)S(1)}, bf16[32,16384]{1,0:T(8,128)(2,1)S(1)}) custom-call(s32[2,16]{1,0:T(2,128)} %bitcast.2, bf16[256,16384]{1,0:T(8,128)(2,1)} %design_ref.1, bf16[32,16384]{1,0:T(8,128)(2,1)} %targets_ref.1, s32[2,16384]{1,0:T(2,128)} %flips_ref.1, s32[2,512]{1,0:T(2,128)} %listed_ref.1), custom_call_target="tpu_custom_call" | custom-call | tf_op jit(solution)/shard_map/sketch_solve/pallas_call | solution.py:539
  40.7 2.4 %residual.1 = (f32[32,256]{1,0:T(8,128)}, f32[32,16384]{1,0:T(8,128)}) custom-call(f32[32,256]{1,0:T(8,128)S(1)} %get-tuple-element.7.solved_ref, bf16[256,16384]{1,0:T(8,128)(2,1)S(1)} %get-tuple-element.8.design_ref, bf16[32,16384]{1,0:T(8,128)(2,1)S(1)} %get-tuple-element.9.targets_ref), custom_call_target="tpu_custom_call" | custom-call | tf_op jit(solution)/shard_map/residual/pallas_call | solution.py:582

commit v5 on v4

--- a/solution.py
+++ b/solution.py
@@ -15,7 +15,6 @@
 NT = (((1,), (1,)), ((), ()))
 TN = (((0,), (0,)), ((), ()))
 NN = (((1,), (0,)), ((), ()))
-HIGHEST = lax.Precision.HIGHEST
 
 
 def parity_sign(bits):
@@ -167,7 +166,10 @@
     rs_e,
     sf,
     ef,
-    mat,
+    cross_ref,
+    own_b,
+    lead_ref,
+    rest_ref,
     gmat,
     bt,
     start_at,
@@ -222,11 +224,10 @@
     for mask in range(1, 64):
         pl.semaphore_signal(barrier, inc=1, device_id=(row ^ mask, col), device_id_type=MESH)
 
-    for k in range(1, 8):
-
-        @pl.when(((z + k) % 8) // 2 != col)
-        def _():
-            pl.semaphore_signal(barrier, inc=1, device_id=z_peer(k), device_id_type=MESH)
+    for mask in range(2, 8):
+        other = z ^ mask
+        peer = ((other % 2) * 32 + row % 32, other // 2)
+        pl.semaphore_signal(barrier, inc=1, device_id=peer, device_id_type=MESH)
 
     small[0].wait()
     small[1].wait()
@@ -423,18 +424,24 @@
         if done == 1:
             all_of(rs_e.at[0:7], 3).wait_recv()
             gather_xy(ef, 5)
+        if done == 6:
+            all_of(sf.at[0:4, 0:15], 16).wait_recv()
+            second_half = half_of(1)
+            cross_ref[...] = product(half_of(0), second_half, TN) * unscale
+            tail[...] = product(second_half, second_half, TN) * unscale + unit
 
     def after_low(done):
         if done == 5:
             all_of(ef.at[:, 0:15], 5).wait_recv()
+            for half in range(2):
+                lanes = slice(half * 128, (half + 1) * 128)
+                for rb in range(8):
+                    own_b[rb * 4 : rb * 4 + 4, lanes] = ef[2 * col + half, rb]
 
             @pl.when(core == 0)
             def _():
-                for half in range(2):
-                    lanes = slice(half * 128, (half + 1) * 128)
-                    for rb in range(8):
-                        bt[rb * 4 : rb * 4 + 4, lanes] = ef[2 * col + half, rb]
-                remote(bt, bt, 15, (row + 1, col)).start()
+                bt[...] = own_b[...]
+                remote(own_b, bt, 15, (row + 1, col)).start()
 
             @pl.when(core == 1)
             def _():
@@ -446,34 +453,37 @@
                             gmat[first : first + 4, lanes] = ef[2 * c + half, rb]
                 remote(gmat, gmat, 18, (row - 1, col)).start()
 
+        if done == 6:
+            lead = own_b[:, 0:128]
+            lead_ref[...] = product(lead, top[...], NN)
+            rest_ref[...] = own_b[:, 128:256] - product(lead, ratio_ref[...], NN)
+
     invert(top, after_top)
-    all_of(sf.at[0:4, 0:15], 16).wait_recv()
-    second_half = half_of(1)
-    cross = product(half_of(0), second_half, TN) * unscale
-    ratio = product(top[...], cross, NN)
-    corner = product(second_half, second_half, TN) * unscale + unit
-    tail[...] = corner - product(cross, ratio, TN)
+    ratio = product(top[...], cross_ref[...], NN)
+    tail[...] = tail[...] - product(cross_ref[...], ratio, TN)
     ratio_ref[...] = ratio
     invert(tail, after_low)
-    ratio = ratio_ref[...]
-    corner = tail[...]
-    across = product(ratio, corner, NN)
-    mat[0:128, 0:128] = (top[...] + product(across, ratio, NT)) * unscale
-    mat[0:128, 128:256] = across * -unscale
-    mat[128:256, 0:128] = product(corner, ratio, NT) * -unscale
-    mat[128:256, 128:256] = corner * unscale
 
     @pl.when(core == 0)
     def _():
-        start_at[...] = product(bt[...], mat[...], NN)
+        rest = product(rest_ref[...], tail[...], NN)
+        lead = lead_ref[...] - product(rest, ratio_ref[...], NT)
+        start_at[:, 0:128] = lead * unscale
+        start_at[:, 128:256] = rest * unscale
         remote(start_at, start_at, 6, (row + 1, col)).start()
         remote(gmat, gmat, 18, (row + 1, col)).wait_recv()
 
     @pl.when(core == 1)
     def _():
-        last[...] = mat[...]
+        ratio = ratio_ref[...]
+        corner = tail[...]
+        across = product(ratio, corner, NN)
+        last[0:128, 0:128] = (top[...] + product(across, ratio, NT)) * unscale
+        last[0:128, 128:256] = across * -unscale
+        last[128:256, 0:128] = product(corner, ratio, NT) * -unscale
+        last[128:256, 128:256] = corner * unscale
         remote(last, last, 7, (row - 1, col)).start()
-        remote(bt, bt, 15, (row - 1, col)).wait_recv()
+        remote(own_b, bt, 15, (row - 1, col)).wait_recv()
         remote(start_at, start_at, 6, (row - 1, col)).wait_recv()
 
     start = start_at[...]
@@ -492,7 +502,7 @@
     @pl.when(core == 0)
     def _():
         remote(start_at, start_at, 6, (row + 1, col)).wait_send()
-        remote(bt, bt, 15, (row + 1, col)).wait_send()
+        remote(own_b, bt, 15, (row + 1, col)).wait_send()
 
     @pl.when(core == 1)
     def _():
@@ -561,7 +571,10 @@
             pltpu.VMEM((63, 4, 128), F32),
             pltpu.VMEM((8, 16, 8, 128), F32),
             pltpu.VMEM((8, 16, 4, 128), F32),
-            pltpu.VMEM((unknowns, unknowns), F32),
+            pltpu.VMEM((128, 128), F32),
+            pltpu.VMEM((rhs, unknowns), F32),
+            pltpu.VMEM((rhs, 128), F32),
+            pltpu.VMEM((rhs, 128), F32),
             pltpu.VMEM((unknowns, unknowns), F32),
             pltpu.VMEM((rhs, unknowns), F32),
             pltpu.VMEM((rhs, unknowns), F32),

time: 43.1 us -> 42.9 us (level)
  no operation moved by 1% of the time
where the time goes in v5:
time: 42.9 us; the launch traced here: 42.8 us
  Pallas kernels  42.2 us (98%)
  between operations  0.64 us (1%)
    pallas_call x1, Pallas kernels, on_device(): pl.pallas_call(kernel, out_shape=(jax.ShapeDtypeStruct((rhs, unknowns), F...  39.8 us
    pallas_call x1, Pallas kernels, on_device(): pl.pallas_call(residual_kernel, out_shape=(jax.ShapeDtypeStruct((rhs, unk...  2.35 us

profile of v5, /device:TPU:1, one launch (start us, length us, event | category | flops | bytes accessed | tf_op | source)
XLA Modules:
  0.0 42.8 jit_solution(2402394322580095189)
XLA Ops:
  0.6 39.8 %sketch_solve.1 = (f32[32,256]{1,0:T(8,128)S(1)}, bf16[256,16384]{1,0:T(8,128)(2,1)S(1)}, bf16[32,16384]{1,0:T(8,128)(2,1)S(1)}) custom-call(s32[2,16]{1,0:T(2,128)} %bitcast.2, bf16[256,16384]{1,0:T(8,128)(2,1)} %design_ref.1, bf16[32,16384]{1,0:T(8,128)(2,1)} %targets_ref.1, s32[2,16384]{1,0:T(2,128)} %flips_ref.1, s32[2,512]{1,0:T(2,128)} %listed_ref.1), custom_call_target="tpu_custom_call" | custom-call | tf_op jit(solution)/shard_map/sketch_solve/pallas_call | solution.py:549
  40.5 2.4 %residual.1 = (f32[32,256]{1,0:T(8,128)}, f32[32,16384]{1,0:T(8,128)}) custom-call(f32[32,256]{1,0:T(8,128)S(1)} %get-tuple-element.7.solved_ref, bf16[256,16384]{1,0:T(8,128)(2,1)S(1)} %get-tuple-element.8.design_ref, bf16[32,16384]{1,0:T(8,128)(2,1)S(1)} %get-tuple-element.9.targets_ref), custom_call_target="tpu_custom_call" | custom-call | tf_op jit(solution)/shard_map/residual/pallas_call | solution.py:595

commit v6 on v5

--- a/solution.py
+++ b/solution.py
@@ -395,21 +395,22 @@
     )
     for mask in plane:
         remote(sums.at[xy], sums.at[xy], 17, (row ^ (2 * mask), col)).start()
-    def send_rest(whose):
+    def send_rest(whose, tiles):
         for parity, second in ((0, odd), (1, even)):
 
             @pl.when((z_lo == parity) & (core == whose))
             def _():
-                for k in second:
+                for k in second[tiles]:
                     over_plane(k, 16)
 
-    send_rest(0)
+    send_rest(0, slice(0, 4))
+    send_rest(1, slice(0, 1))
     all_of(rs_e, 1).wait_recv()
     ef[z, xy] = total(xe[row], rs_e)
     gather_z(ef, 3)
     all_of(sf.at[0:4, 0:15], 4).wait_recv()
     all_of(sums.at[0:15], 17).wait_recv()
-    send_rest(1)
+    send_rest(1, slice(1, 4))
 
     def half_of(half):
         return jnp.concatenate([sf[2 * c + half].reshape(picks, 128) for c in range(4)], axis=0)

time: 42.9 us -> 42.9 us (level)
  no operation moved by 1% of the time
where the time goes in v6:
time: 42.9 us; the launch traced here: 42.8 us
  Pallas kernels  42.2 us (98%)
  between operations  0.64 us (1%)
    pallas_call x1, Pallas kernels, on_device(): pl.pallas_call(kernel, out_shape=(jax.ShapeDtypeStruct((rhs, unknowns), F...  39.8 us
    pallas_call x1, Pallas kernels, on_device(): pl.pallas_call(residual_kernel, out_shape=(jax.ShapeDtypeStruct((rhs, unk...  2.35 us

profile of v6, /device:TPU:1, one launch (start us, length us, event | category | flops | bytes accessed | tf_op | source)
XLA Modules:
  0.0 42.8 jit_solution(15429119540057871222)
XLA Ops:
  0.6 39.8 %sketch_solve.1 = (f32[32,256]{1,0:T(8,128)S(1)}, bf16[256,16384]{1,0:T(8,128)(2,1)S(1)}, bf16[32,16384]{1,0:T(8,128)(2,1)S(1)}) custom-call(s32[2,16]{1,0:T(2,128)} %bitcast.2, bf16[256,16384]{1,0:T(8,128)(2,1)} %design_ref.1, bf16[32,16384]{1,0:T(8,128)(2,1)} %targets_ref.1, s32[2,16384]{1,0:T(2,128)} %flips_ref.1, s32[2,512]{1,0:T(2,128)} %listed_ref.1), custom_call_target="tpu_custom_call" | custom-call | tf_op jit(solution)/shard_map/sketch_solve/pallas_call | solution.py:550
  40.5 2.4 %residual.1 = (f32[32,256]{1,0:T(8,128)}, f32[32,16384]{1,0:T(8,128)}) custom-call(f32[32,256]{1,0:T(8,128)S(1)} %get-tuple-element.7.solved_ref, bf16[256,16384]{1,0:T(8,128)(2,1)S(1)} %get-tuple-element.8.design_ref, bf16[32,16384]{1,0:T(8,128)(2,1)S(1)} %get-tuple-element.9.targets_ref), custom_call_target="tpu_custom_call" | custom-call | tf_op jit(solution)/shard_map/residual/pallas_call | solution.py:596
